TPU v7x, 256 devices: a whole 4x4x8 slice. The times are simulated.
256 devices in a mesh: req: 64 (over z, x, core), tp: 4 (over y).
Axes of the slice: x: 4, y: 4, z: 8, core: 2. Of those that a mesh axis runs over, the one named last changes fastest.
Arguments:
- hidden_in: bfloat16 [32768, 1024], P('req', 'tp'), may hold values from -6 to 6
- w_qkv: bfloat16 [1024, 3, 1024], P(None, None, 'tp'), may hold values from -0.1875 to 0.1875
- w_out: bfloat16 [1024, 1024], P('tp'), may hold values from -0.75 to 0.75
- first_gain: float32 [1024], replicated, may hold values from 0.1 to 1.9
- w_up: bfloat16 [1024, 4096], P(None, 'tp'), may hold values from -0.1875 to 0.1875
- w_down: bfloat16 [4096, 1024], P('tp'), may hold values from -0.09375 to 0.09375
- second_gain: float32 [1024], replicated, may hold values from 0.1 to 1.9
- cache_pool: bfloat16 [4096, 128, 2, 1024], P('req', None, None, 'tp'), may hold values from -600 to 600
- page_table: int32 [512, 8], P('req'), may hold values from 0 to 63, as said below
- cache_len: int32 [512], P('req'), may hold values from 1 to 1024, as said below
- tree_parent: int32 [512, 64], P('req'), may hold values from -1 to 62, as said below
- accept_node: int32 [512], P('req'), may hold values from 0 to 63
Outputs:
- layer_out: bfloat16 [32768, 1024], P('req', 'tp')
- accepted_kv: bfloat16 [512, 64, 2, 1024], P('req', None, None, 'tp')
Inputs may be any that keep to these rules, and one draw needn't show every extreme that they name: `page_table`: on each index e of req, the 8 x 8 entries of its rows are a permutation of the slots 0 to 63; row j, column m holds the slot in e's pool of page j of member m of the index e - j of req (modulo the axis size). `cache_len`: on each index of req exactly 2 requests have lengths over 256, and the others at most 256; the length 1024 occurs in every draw, and so does the length 256. `tree_parent`: node 0 is the root with parent -1; every other node's parent is an earlier node.
All inputs are finite; a program needn't handle non-finite values.
Results may differ from a plain program's by a relative error of at most 0.012.
Values may be sent and summed in bfloat16 or wider, within the bound.
A program may use at most 128 MiB of HBM per device.

v0:
```python
import jax
import jax.numpy as jnp
from jax import lax
from jax.sharding import PartitionSpec as P

HD = 64
NEG = -1e30
EPS = 1e-05


def from_behind(value, axis, by):
    size = lax.axis_size(axis)
    return lax.ppermute(value, axis, [(i, (i + by) % size) for i in range(size)])


def block_partial(queries, key_rows, value_rows, valid):
    scores = jnp.einsum("bqhd,bkhd->bhqk", queries, key_rows, preferred_element_type=jnp.float32)
    allowed = valid[:, None, :, :]
    maxima = jnp.max(jnp.where(allowed, scores, NEG), axis=-1)
    weights = jnp.where(allowed, jnp.exp(scores - maxima[..., None]), 0.0).astype(jnp.bfloat16)
    totals = jnp.sum(weights.astype(jnp.float32), axis=-1)
    mixture = jnp.einsum("bhqk,bkhd->bqhd", weights, value_rows, preferred_element_type=jnp.float32)
    return (mixture, maxima, totals)


def combine_blocks(mixture, maxima, totals):
    best = jnp.max(maxima, axis=0)
    scale = jnp.swapaxes(jnp.exp(maxima - best[None]), -1, -2)
    numer = jnp.sum(mixture * scale[..., None], axis=0)
    denom = jnp.sum(jnp.swapaxes(totals, -1, -2) * scale, axis=0)
    return numer / denom[..., None]


def ancestors(parents):
    count = parents.shape[-1]
    reach = jax.nn.one_hot(parents, count, dtype=jnp.float32) + jnp.eye(count, dtype=jnp.float32)
    for sweep in range(max(1, (count - 1).bit_length())):
        reach = jnp.minimum(
            jnp.einsum("rij,rjk->rik", reach, reach, precision=lax.Precision.HIGHEST), 1.0
        )
    return reach


def page_rows(cache_pool, slot_ids):
    picker = jax.nn.one_hot(slot_ids, cache_pool.shape[0], dtype=jnp.bfloat16)
    return jnp.einsum(
        "rs,spcf->rpcf", picker, cache_pool, preferred_element_type=jnp.float32
    ).astype(jnp.bfloat16)


def rows_split(rows, heads_local):
    requests, page_len = (rows.shape[0], rows.shape[1])
    return (
        rows[:, :, 0].reshape(requests, page_len, heads_local, HD),
        rows[:, :, 1].reshape(requests, page_len, heads_local, HD),
    )


def page_split(cache_pool, slot_ids, heads_local):
    return rows_split(page_rows(cache_pool, slot_ids), heads_local)


def spread_back(arrived, long_ids, requests):
    mixture = (
        jnp.zeros((requests,) + arrived[0].shape[1:], jnp.float32).at[long_ids].set(arrived[0])
    )
    maxima = (
        jnp.full((requests,) + arrived[1].shape[1:], NEG, jnp.float32).at[long_ids].set(arrived[1])
    )
    totals = jnp.zeros((requests,) + arrived[2].shape[1:], jnp.float32).at[long_ids].set(arrived[2])
    return (mixture, maxima, totals)


def norm_from_sums(values, sums, gain, width_all):
    center = (sums[0] / width_all)[:, None]
    spread = (sums[1] / width_all)[:, None] - center * center
    return (values - center) * lax.rsqrt(spread + EPS) * gain


def shards(
    hidden_in,
    w_qkv,
    w_out,
    first_gain,
    w_up,
    w_down,
    second_gain,
    cache_pool,
    page_table,
    cache_len,
    tree_parent,
    accept_node,
):
    tokens_dev, share = hidden_in.shape
    requests, draft = tree_parent.shape
    width_local = w_qkv.shape[2]
    heads_local = width_local // HD
    page_count = page_table.shape[0]
    page_len = cache_pool.shape[1]
    width_all = share * lax.axis_size("tp")
    start = lax.axis_index("tp") * share
    gathered = lax.all_gather(hidden_in, "tp", axis=1, tiled=True)
    projected = jnp.einsum("td,dcf->tcf", gathered, w_qkv, preferred_element_type=jnp.float32)
    queries = (
        (projected[:, 0] * 0.125).astype(jnp.bfloat16).reshape(requests, draft, heads_local, HD)
    )
    key_new = projected[:, 1].astype(jnp.bfloat16)
    value_new = projected[:, 2].astype(jnp.bfloat16)
    key_heads = key_new.reshape(requests, draft, heads_local, HD)
    value_heads = value_new.reshape(requests, draft, heads_local, HD)
    reach = ancestors(tree_parent)
    long_count = (requests + 3) // 4
    is_long = (cache_len > 2 * page_len).astype(jnp.int32)
    rank_score = is_long * (2 * requests) + (requests - jnp.arange(requests, dtype=jnp.int32))
    ranked, long_ids = lax.top_k(rank_score, long_count)
    long_queries = queries[long_ids]
    member_code = long_ids.astype(jnp.bfloat16)
    parts = [block_partial(queries, key_heads, value_heads, reach > 0.5)]
    positions = jnp.arange(page_len, dtype=jnp.int32)
    for page_index in range(page_count):
        valid_rows = page_index * page_len + positions[None, :] < cache_len[:, None]
        valid = jnp.broadcast_to(valid_rows[:, None, :], (requests, draft, page_len))
        if page_index == 0:
            key_rows, value_rows = page_split(cache_pool, page_table[0], heads_local)
            result = block_partial(queries, key_rows, value_rows, valid)
        elif page_index == 1:
            incoming, flags = from_behind(
                (queries, valid_rows.astype(jnp.bfloat16)), "req", page_index
            )
            key_rows, value_rows = page_split(cache_pool, page_table[page_index], heads_local)
            remote_valid = jnp.broadcast_to((flags > 0.5)[:, None, :], (requests, draft, page_len))
            remote = block_partial(incoming, key_rows, value_rows, remote_valid)
            result = from_behind((remote[0], remote[1], remote[2]), "req", -page_index)
        else:
            long_flags = valid_rows[long_ids].astype(jnp.bfloat16)
            incoming, flags, members = from_behind(
                (long_queries, long_flags, member_code), "req", page_index
            )
            member_ids = members.astype(jnp.int32)
            key_rows, value_rows = page_split(
                cache_pool, page_table[page_index][member_ids], heads_local
            )
            remote_valid = jnp.broadcast_to(
                (flags > 0.5)[:, None, :], (long_count, draft, page_len)
            )
            remote = block_partial(incoming, key_rows, value_rows, remote_valid)
            arrived = from_behind((remote[0], remote[1], remote[2]), "req", -page_index)
            result = spread_back(arrived, long_ids, requests)
        parts.append(result)
    mixture = jnp.stack([piece[0] for piece in parts], axis=0)
    maxima = jnp.stack([piece[1] for piece in parts], axis=0)
    totals = jnp.stack([piece[2] for piece in parts], axis=0)
    attended = (
        combine_blocks(mixture, maxima, totals)
        .reshape(tokens_dev, width_local)
        .astype(jnp.bfloat16)
    )
    branch = jnp.dot(attended, w_out, preferred_element_type=jnp.float32)
    second_share = lax.dynamic_slice_in_dim(second_gain, start, share, 0)
    summed = lax.psum(branch, "tp")
    mixed_all = gathered.astype(jnp.float32) + summed
    whole_sums = (jnp.sum(mixed_all, axis=-1), jnp.sum(mixed_all * mixed_all, axis=-1))
    normed_all = norm_from_sums(mixed_all, whole_sums, first_gain, width_all).astype(jnp.bfloat16)
    normed_share = lax.dynamic_slice_in_dim(normed_all, start, share, 1)
    inner = jax.nn.gelu(
        jnp.dot(normed_all, w_up, preferred_element_type=jnp.float32), approximate=False
    ).astype(jnp.bfloat16)
    outer = lax.psum_scatter(
        jnp.dot(inner, w_down, preferred_element_type=jnp.float32).astype(jnp.bfloat16),
        "tp",
        scatter_dimension=1,
        tiled=True,
    ).astype(jnp.float32)
    second_in = normed_share.astype(jnp.float32) + outer
    second_sums = lax.psum(
        (jnp.sum(second_in, axis=-1), jnp.sum(second_in * second_in, axis=-1)), "tp"
    )
    layer_out = norm_from_sums(second_in, second_sums, second_share, width_all).astype(jnp.bfloat16)
    pairs = jnp.stack(
        [
            key_new.reshape(requests, draft, width_local),
            value_new.reshape(requests, draft, width_local),
        ],
        axis=2,
    )
    depth = jnp.sum(reach, axis=-1) - 1.0
    chosen = jnp.einsum(
        "rq,rqk->rk",
        jax.nn.one_hot(accept_node, draft, dtype=jnp.float32),
        reach,
        precision=lax.Precision.HIGHEST,
    )
    levels = jnp.arange(draft, dtype=jnp.float32)
    select = (
        chosen[:, None, :] * (depth[:, None, :] == levels[None, :, None]).astype(jnp.float32)
    ).astype(jnp.bfloat16)
    accepted_kv = jnp.einsum(
        "rsk,rkcf->rscf", select, pairs, preferred_element_type=jnp.float32
    ).astype(jnp.bfloat16)
    return (layer_out, accepted_kv)


def solution(mesh):
    placed = (
        P("req", "tp"),
        P(None, None, "tp"),
        P("tp", None),
        P(),
        P(None, "tp"),
        P("tp", None),
        P(),
        P("req", None, None, "tp"),
        P("req", None),
        P("req"),
        P("req", None),
        P("req"),
    )
    return jax.shard_map(
        shards,
        mesh=mesh,
        in_specs=placed,
        out_specs=(P("req", "tp"), P("req", None, None, "tp")),
        check_vma=False,
    )
```

profile of v0, /device:TPU:2, one launch (start us, length us, event | category | flops | bytes accessed | tf_op | source)
XLA Modules:
  0.0 424.8 jit_solution(16485412989436485535)
XLA Ops:
  11.1 4.3 %collective-permute-start.15 = (bf16[2]{0:T(256)(128)(2,1)S(1)}, bf16[2]{0:T(256)(128)(2,1)S(1)}, u32[]{:S(2)}, u32[]{:S(2)}) collective-permute-start(bf16[2]{0:T(256)(128)(2,1)S(1)} %get-tuple-element.60), channel_id=1, source_target_pairs={{0,20},{4,24},{8,28},{12,32},{16,36},{20,40},{24,44},{28,48},{32,5... | collective-permute-start | bytes 20 | tf_op jit(solution)/shard_map/ppermute | solution.py:13
  21.2 7.9 %convolution_convert_fusion.2 = bf16[8,128,2,256]{3,0,2,1:T(8,128)(2,1)S(1)} fusion(bf16[64,128,2,256]{3,2,1,0:T(2,128)(2,1)} %param.19, s32[8]{0:T(128)S(1)} %get-tuple-element.46), kind=kOutput, calls=%fused_computation.56 | convolution fusion | flops 67633664 | bytes 9437216 | tf_op jit(solution)/shard_map/rs,spcf->rpcf/dot_general | solution.py:46
  31.6 2.3 copy.165
  33.9 8.4 %convolution_convert_fusion.1 = bf16[8,128,2,256]{3,0,2,1:T(8,128)(2,1)S(1)} fusion(bf16[64,128,2,256]{3,2,1,0:T(2,128)(2,1)} %param.19, s32[8]{0:T(128)S(1)} %get-tuple-element.45), kind=kOutput, calls=%fused_computation.55 | convolution fusion | flops 67633664 | bytes 9437216 | tf_op jit(solution)/shard_map/rs,spcf->rpcf/dot_general | solution.py:46
  43.3 2.2 copy.168
  45.5 2.2 copy.170
  51.3 2.9 collective-permute-start.19
  55.3 8.0 %fusion.26 = bf16[2,128,2,256]{3,0,2,1:T(2,128)(2,1)S(1)} fusion(bf16[64,128,2,256]{3,2,1,0:T(2,128)(2,1)} %param.19, s32[2]{0:T(128)S(1)} %gather_fusion), kind=kOutput, calls=%fused_computation.77 | convolution fusion | flops 16908416 | bytes 8650760 | tf_op jit(solution)/shard_map/rs,spcf->rpcf/dot_general | solution.py:46
  64.8 8.0 %fusion.29 = bf16[2,128,2,256]{3,0,2,1:T(2,128)(2,1)S(1)} fusion(bf16[64,128,2,256]{3,2,1,0:T(2,128)(2,1)} %param.19, s32[2]{0:T(128)S(1)} %gather_fusion.3), kind=kOutput, calls=%fused_computation.78 | convolution fusion | flops 16908416 | bytes 8650760 | tf_op jit(solution)/shard_map/rs,spcf->rpcf/dot_general | solution.py:46
  73.7 2.4 collective-permute-start.4
  76.1 3.1 collective-permute-start.8
  79.9 8.0 %fusion.32 = bf16[2,128,2,256]{3,0,2,1:T(2,128)(2,1)S(1)} fusion(bf16[64,128,2,256]{3,2,1,0:T(2,128)(2,1)} %param.19, s32[2]{0:T(128)S(1)} %gather_fusion.5), kind=kOutput, calls=%fused_computation.79 | convolution fusion | flops 16908416 | bytes 8650760 | tf_op jit(solution)/shard_map/rs,spcf->rpcf/dot_general | solution.py:46
  89.4 8.0 %fusion.35 = bf16[2,128,2,256]{3,0,2,1:T(2,128)(2,1)S(1)} fusion(bf16[64,128,2,256]{3,2,1,0:T(2,128)(2,1)} %param.19, s32[2]{0:T(128)S(1)} %gather_fusion.7), kind=kOutput, calls=%fused_computation.80 | convolution fusion | flops 16908416 | bytes 8650760 | tf_op jit(solution)/shard_map/rs,spcf->rpcf/dot_general | solution.py:46
  98.3 2.0 collective-permute-start.12
  100.4 3.7 collective-permute-start.16
  104.7 8.0 %fusion.38 = bf16[2,128,2,256]{3,0,2,1:T(2,128)(2,1)S(1)} fusion(bf16[64,128,2,256]{3,2,1,0:T(2,128)(2,1)} %param.19, s32[2]{0:T(128)S(1)} %gather_fusion.9), kind=kOutput, calls=%fused_computation.81 | convolution fusion | flops 16908416 | bytes 8650760 | tf_op jit(solution)/shard_map/rs,spcf->rpcf/dot_general | solution.py:46
  114.2 8.0 %fusion.41 = bf16[2,128,2,256]{3,0,2,1:T(2,128)(2,1)S(1)} fusion(bf16[64,128,2,256]{3,2,1,0:T(2,128)(2,1)} %param.19, s32[2]{0:T(128)S(1)} %gather_fusion.11), kind=kOutput, calls=%fused_computation.82 | convolution fusion | flops 16908416 | bytes 8650760 | tf_op jit(solution)/shard_map/rs,spcf->rpcf/dot_general | solution.py:46
  124.7 1.7 copy.178
  127.2 1.7 copy.183
  128.9 1.7 copy.184
  130.5 1.7 copy.188
  132.2 1.7 copy.189
  133.9 1.7 copy.193
  135.6 1.7 copy.194
  138.8 1.8 collective-permute-start.24
  140.7 3.8 collective-permute-done.20
  144.5 2.7 fusion.45
  151.0 2.3 gather_fusion.2
  154.7 2.2 collective-permute-start.13
  159.1 2.0 convert_element_type.221
  161.1 2.0 convert_element_type.227
  163.2 1.5 select_reduce_fusion.2
  172.9 2.1 collective-permute-start.35
  176.8 2.9 collective-permute-start.36
  182.2 3.0 collective-permute-start.37
  189.3 3.0 collective-permute-start.39
  193.5 4.2 collective-permute-start.29
  198.5 4.0 collective-permute-start.40
  204.2 3.1 collective-permute-start.32
  210.9 2.2 collective-permute-start.14
  213.4 4.9 %collective-permute-done.6 = f32[2,64,4,64]{1,3,2,0:T(8,128)S(1)} collective-permute-done((f32[2,64,4,64]{1,3,2,0:T(8,128)S(1)}, f32[2,64,4,64]{1,3,2,0:T(8,128)S(1)}, u32[]{:S(2)}, u32[]{:S(2)}) %collective-permute-start.6) | collective-permute-done | bytes 131104 | tf_op jit(solution)/shard_map/ppermute | solution.py:13
  218.3 4.8 %collective-permute-start.22 = (f32[2,64,4,64]{1,3,2,0:T(8,128)}, f32[2,64,4,64]{1,3,2,0:T(8,128)}, u32[]{:S(2)}, u32[]{:S(2)}) collective-permute-start(f32[2,64,4,64]{1,3,2,0:T(8,128)} %convolution_bitcast_fusion.4), channel_id=1, source_target_pairs={{0,232},{4,236},{8,240},{12,244},{16,248},{20,252},{24,0},{28,4},{... | collective-permute-start | bytes 393224 | tf_op jit(solution)/shard_map/ppermute | solution.py:13
  233.5 1.5 scatter_fusion
  236.4 1.8 copy.180
  238.3 1.5 scatter_fusion.1
  241.2 1.8 copy.185
  243.1 1.5 scatter_fusion.2
  246.0 1.8 copy.190
  247.9 1.5 scatter_fusion.3
  250.8 1.8 copy.195
  252.7 1.5 scatter_fusion.4
  255.6 1.8 copy.200
  257.5 1.5 scatter_fusion.5
  260.4 1.8 select_reduce_fusion
  265.7 4.7 %collective-permute-start.2 = (f32[8,64,4,64]{1,3,2,0:T(8,128)S(1)}, f32[8,64,4,64]{1,3,2,0:T(8,128)S(1)}, u32[]{:S(2)}, u32[]{:S(2)}) collective-permute-start(f32[8,64,4,64]{1,3,2,0:T(8,128)S(1)} %convolution_bitcast_fusion), channel_id=1, source_target_pairs={{0,252},{4,0},{8,4},{12,8},{16,12},{20,16},{24,20},{28,24},{32,28}... | collective-permute-start | bytes 1572872 | tf_op jit(solution)/shard_map/ppermute | solution.py:13
  275.7 7.0 %collective-permute-done.2 = f32[8,64,4,64]{1,3,2,0:T(8,128)S(1)} collective-permute-done((f32[8,64,4,64]{1,3,2,0:T(8,128)S(1)}, f32[8,64,4,64]{1,3,2,0:T(8,128)S(1)}, u32[]{:S(2)}, u32[]{:S(2)}) %collective-permute-start.2) | collective-permute-done | bytes 524320 | tf_op jit(solution)/shard_map/ppermute | solution.py:13
  290.5 5.6 %multiply_reduce_fusion = f32[8,64,4,64]{1,3,2,0:T(8,128)S(1)} fusion(f32[9,8,64,4,64]{2,4,3,1,0:T(8,128)} %bitcast_dynamic-update-slice_fusion, f32[9,8,64,4]{2,3,1,0:T(4,128)S(1)} %get-tuple-element.21), kind=kLoop, calls=%fused_computation.31 | loop fusion | flops 2228224 | bytes 5316608 | tf_op jit(solution)/shard_map/reduce_sum | solution.py:29
  297.6 3.0 fusion.186
  300.6 66.8 %all-reduce.3.cloned.1.call-done = f32[512,1024]{1,0:T(8,128)} async-done(((f32[512,1024]{1,0:T(8,128)}), f32[512,1024]{1,0:T(8,128)}) %all-reduce.3.cloned.1.call-update) | async-done | bytes 2097168 | tf_op jit(solution)/shard_map/psum | solution.py:160
  367.4 2.2 fusion.77
  371.1 9.2 %convolution_convert_fusion = bf16[512,1024]{1,0:T(8,128)(2,1)} fusion(bf16[1024,1024]{1,0:T(8,128)(2,1)S(1)} %copy-done, bf16[512,1024]{1,0:T(8,128)(2,1)} %multiply_convert_fusion, bf16[1024,1024]{1,0:T(8,128)(2,1)} %param.16), kind=kOutput, calls=%fused_computation.54 | convolution fusion | flops 2182086656 | bytes 6291456 | tf_op jit(solution)/shard_map/dot_general | solution.py:169
  384.2 22.1 %reduce-scatter.2.cloned.1.call-done = bf16[512,256]{1,0:T(8,128)(2,1)} async-done(((bf16[512,1024]{1,0:T(8,128)(2,1)}), bf16[512,256]{1,0:T(8,128)(2,1)}) %reduce-scatter.2.cloned.1.call-update) | async-done | bytes 262160 | tf_op jit(solution)/shard_map/reduce_scatter | solution.py:168
  407.5 8.5 %all-reduce = (f32[512]{0:T(512)S(1)}, f32[512]{0:T(512)S(1)}) all-reduce(f32[512]{0:T(512)S(1)} %get-tuple-element.17, f32[512]{0:T(512)S(1)} %get-tuple-element.16), channel_id=1, replica_groups=mesh['req'=64,'tp'=4] {'tp'}, use_global_device_ids=true, to_apply=%region_46.47 | all-reduce | flops 1024 | bytes 8192 | tf_op jit(solution)/shard_map/psum | solution.py:175
  416.0 1.9 multiply_convert_fusion.1
  (338 shorter events, 105.1 us)
Async XLA Ops:
  7.2 363.9 %copy-start = (bf16[1024,1024]{1,0:T(8,128)(2,1)S(1)}, bf16[1024,1024]{1,0:T(8,128)(2,1)}, u32[]{:S(2)}) copy-start(bf16[1024,1024]{1,0:T(8,128)(2,1)} %param.17) | copy-start | bytes 6291460
  7.2 137.3 %all-gather.2.cloned.1.call-start = ((), (), s32[]{:S(2)}) async-start(), calls=%async_computation.1 | async-start | bytes 1310720 | tf_op jit(solution)/shard_map/all_gather | solution.py:102
  9.0 42.3 %collective-permute-start.7 = (bf16[2]{0:T(256)(128)(2,1)S(1)}, bf16[2]{0:T(256)(128)(2,1)S(1)}, u32[]{:S(2)}, u32[]{:S(2)}) collective-permute-start(bf16[2]{0:T(256)(128)(2,1)S(1)} %get-tuple-element.60), channel_id=1, source_target_pairs={{0,12},{4,16},{8,20},{12,24},{16,28},{20,32},{24,36},{28,40},{32,4... | collective-permute-start | bytes 20 | tf_op jit(solution)/shard_map/ppermute | solution.py:13
  9.9 44.3 %collective-permute-start.3 = (bf16[2]{0:T(256)(128)(2,1)S(1)}, bf16[2]{0:T(256)(128)(2,1)S(1)}, u32[]{:S(2)}, u32[]{:S(2)}) collective-permute-start(bf16[2]{0:T(256)(128)(2,1)S(1)} %get-tuple-element.60), channel_id=1, source_target_pairs={{0,8},{4,12},{8,16},{12,20},{16,24},{20,28},{24,32},{28,36},{32,40... | collective-permute-start | bytes 20 | tf_op jit(solution)/shard_map/ppermute | solution.py:13
  11.1 62.6 %collective-permute-start.15 = (bf16[2]{0:T(256)(128)(2,1)S(1)}, bf16[2]{0:T(256)(128)(2,1)S(1)}, u32[]{:S(2)}, u32[]{:S(2)}) collective-permute-start(bf16[2]{0:T(256)(128)(2,1)S(1)} %get-tuple-element.60), channel_id=1, source_target_pairs={{0,20},{4,24},{8,28},{12,32},{16,36},{20,40},{24,44},{28,48},{32,5... | collective-permute-start | bytes 20 | tf_op jit(solution)/shard_map/ppermute | solution.py:13
  15.4 60.7 %collective-permute-start.11 = (bf16[2]{0:T(256)(128)(2,1)S(1)}, bf16[2]{0:T(256)(128)(2,1)S(1)}, u32[]{:S(2)}, u32[]{:S(2)}) collective-permute-start(bf16[2]{0:T(256)(128)(2,1)S(1)} %get-tuple-element.60), channel_id=1, source_target_pairs={{0,16},{4,20},{8,24},{12,28},{16,32},{20,36},{24,40},{28,44},{32,4... | collective-permute-start | bytes 20 | tf_op jit(solution)/shard_map/ppermute | solution.py:13
  16.7 81.7 %collective-permute-start.23 = (bf16[2]{0:T(256)(128)(2,1)S(1)}, bf16[2]{0:T(256)(128)(2,1)S(1)}, u32[]{:S(2)}, u32[]{:S(2)}) collective-permute-start(bf16[2]{0:T(256)(128)(2,1)S(1)} %get-tuple-element.60), channel_id=1, source_target_pairs={{0,28},{4,32},{8,36},{12,40},{16,44},{20,48},{24,52},{28,56},{32,6... | collective-permute-start | bytes 20 | tf_op jit(solution)/shard_map/ppermute | solution.py:13
  17.4 350.0 %all-reduce.3.cloned.1.call-start = ((), (), s32[]{:S(2)}) async-start(), calls=%async_computation.2 | async-start | bytes 4194304 | tf_op jit(solution)/shard_map/psum | solution.py:160
  51.3 49.1 %collective-permute-start.19 = (bf16[2]{0:T(256)(128)(2,1)S(1)}, bf16[2]{0:T(256)(128)(2,1)S(1)}, u32[]{:S(2)}, u32[]{:S(2)}) collective-permute-start(bf16[2]{0:T(256)(128)(2,1)S(1)} %get-tuple-element.60), channel_id=1, source_target_pairs={{0,24},{4,28},{8,32},{12,36},{16,40},{20,44},{24,48},{28,52},{32,5... | collective-permute-start | bytes 20 | tf_op jit(solution)/shard_map/ppermute | solution.py:13
  54.2 90.3 %collective-permute-start = (bf16[8,128]{1,0:T(8,128)(2,1)S(1)}, bf16[8,128]{1,0:T(8,128)(2,1)S(1)}, u32[]{:S(2)}, u32[]{:S(2)}) collective-permute-start(bf16[8,128]{1,0:T(8,128)(2,1)S(1)} %get-tuple-element.53), channel_id=1, source_target_pairs={{0,4},{4,8},{8,12},{12,16},{16,20},{20,24},{24,28},{28,32},{32,36}... | collective-permute-start | bytes 6152 | tf_op jit(solution)/shard_map/ppermute | solution.py:13
  73.7 65.1 %collective-permute-start.4 = (bf16[2,128]{1,0:T(2,128)(2,1)S(1)}, bf16[2,128]{1,0:T(2,128)(2,1)S(1)}, u32[]{:S(2)}, u32[]{:S(2)}) collective-permute-start(bf16[2,128]{1,0:T(2,128)(2,1)S(1)} %convert_element_type.237), channel_id=1, source_target_pairs={{0,8},{4,12},{8,16},{12,20},{16,24},{20,28},{24,32},{28,36},{32,40... | collective-permute-start | bytes 1544 | tf_op jit(solution)/shard_map/ppermute | solution.py:13
  76.1 62.7 %collective-permute-start.8 = (bf16[2,128]{1,0:T(2,128)(2,1)S(1)}, bf16[2,128]{1,0:T(2,128)(2,1)S(1)}, u32[]{:S(2)}, u32[]{:S(2)}) collective-permute-start(bf16[2,128]{1,0:T(2,128)(2,1)S(1)} %convert_element_type.241), channel_id=1, source_target_pairs={{0,12},{4,16},{8,20},{12,24},{16,28},{20,32},{24,36},{28,40},{32,4... | collective-permute-start | bytes 1544 | tf_op jit(solution)/shard_map/ppermute | solution.py:13
  98.3 42.3 %collective-permute-start.12 = (bf16[2,128]{1,0:T(2,128)(2,1)S(1)}, bf16[2,128]{1,0:T(2,128)(2,1)S(1)}, u32[]{:S(2)}, u32[]{:S(2)}) collective-permute-start(bf16[2,128]{1,0:T(2,128)(2,1)S(1)} %convert_element_type.245), channel_id=1, source_target_pairs={{0,16},{4,20},{8,24},{12,28},{16,32},{20,36},{24,40},{28,44},{32,4... | collective-permute-start | bytes 1544 | tf_op jit(solution)/shard_map/ppermute | solution.py:13
  100.4 40.3 %collective-permute-start.16 = (bf16[2,128]{1,0:T(2,128)(2,1)S(1)}, bf16[2,128]{1,0:T(2,128)(2,1)S(1)}, u32[]{:S(2)}, u32[]{:S(2)}) collective-permute-start(bf16[2,128]{1,0:T(2,128)(2,1)S(1)} %convert_element_type.249), channel_id=1, source_target_pairs={{0,20},{4,24},{8,28},{12,32},{16,36},{20,40},{24,44},{28,48},{32,5... | collective-permute-start | bytes 1544 | tf_op jit(solution)/shard_map/ppermute | solution.py:13
  114.2 12.2 %copy-start.26 = (bf16[2,128,1,256]{3,0,2,1:T(2,128)(2,1)S(1)}, bf16[2,128,1,256]{3,0,2,1:T(2,128)(2,1)}, u32[]{:S(2)}) copy-start(bf16[2,128,1,256]{3,0,2,1:T(2,128)(2,1)} %get-tuple-element.36) | copy-start | bytes 393220
  123.9 14.1 %copy-start.27 = (bf16[2,128,1,256]{3,0,2,1:T(2,128)(2,1)S(1)}, bf16[2,128,1,256]{3,0,2,1:T(2,128)(2,1)}, u32[]{:S(2)}) copy-start(bf16[2,128,1,256]{3,0,2,1:T(2,128)(2,1)} %get-tuple-element.28) | copy-start | bytes 393220
  124.7 12.5 %copy-start.28 = (bf16[2,128,1,256]{3,0,2,1:T(2,128)(2,1)S(1)}, bf16[2,128,1,256]{3,0,2,1:T(2,128)(2,1)}, u32[]{:S(2)}) copy-start(bf16[2,128,1,256]{3,0,2,1:T(2,128)(2,1)} %get-tuple-element.29) | copy-start | bytes 393220
  138.8 5.7 %collective-permute-start.20 = (bf16[2,128]{1,0:T(2,128)(2,1)S(1)}, bf16[2,128]{1,0:T(2,128)(2,1)S(1)}, u32[]{:S(2)}, u32[]{:S(2)}) collective-permute-start(bf16[2,128]{1,0:T(2,128)(2,1)S(1)} %convert_element_type.253), channel_id=1, source_target_pairs={{0,24},{4,28},{8,32},{12,36},{16,40},{20,44},{24,48},{28,52},{32,5... | collective-permute-start | bytes 1544 | tf_op jit(solution)/shard_map/ppermute | solution.py:13
  138.8 5.6 %collective-permute-start.24 = (bf16[2,128]{1,0:T(2,128)(2,1)S(1)}, bf16[2,128]{1,0:T(2,128)(2,1)S(1)}, u32[]{:S(2)}, u32[]{:S(2)}) collective-permute-start(bf16[2,128]{1,0:T(2,128)(2,1)S(1)} %convert_element_type.257), channel_id=1, source_target_pairs={{0,28},{4,32},{8,36},{12,40},{16,44},{20,48},{24,52},{28,56},{32,6... | collective-permute-start | bytes 1544 | tf_op jit(solution)/shard_map/ppermute | solution.py:13
  153.2 17.6 %collective-permute-start.5 = (bf16[2,64,4,64]{3,1,2,0:T(8,128)(2,1)}, bf16[2,64,4,64]{3,1,2,0:T(8,128)(2,1)}, u32[]{:S(2)}, u32[]{:S(2)}) collective-permute-start(bf16[2,64,4,64]{3,1,2,0:T(8,128)(2,1)} %gather_fusion.2), channel_id=1, source_target_pairs={{0,8},{4,12},{8,16},{12,20},{16,24},{20,28},{24,32},{28,36},{32,40... | collective-permute-start | bytes 196616 | tf_op jit(solution)/shard_map/ppermute | solution.py:13
  154.7 18.2 %collective-permute-start.9 = (bf16[2,64,4,64]{3,1,2,0:T(8,128)(2,1)}, bf16[2,64,4,64]{3,1,2,0:T(8,128)(2,1)}, u32[]{:S(2)}, u32[]{:S(2)}) collective-permute-start(bf16[2,64,4,64]{3,1,2,0:T(8,128)(2,1)} %gather_fusion.2), channel_id=1, source_target_pairs={{0,12},{4,16},{8,20},{12,24},{16,28},{20,32},{24,36},{28,40},{32,4... | collective-permute-start | bytes 196616 | tf_op jit(solution)/shard_map/ppermute | solution.py:13
  154.7 22.1 %collective-permute-start.13 = (bf16[2,64,4,64]{3,1,2,0:T(8,128)(2,1)}, bf16[2,64,4,64]{3,1,2,0:T(8,128)(2,1)}, u32[]{:S(2)}, u32[]{:S(2)}) collective-permute-start(bf16[2,64,4,64]{3,1,2,0:T(8,128)(2,1)} %gather_fusion.2), channel_id=1, source_target_pairs={{0,16},{4,20},{8,24},{12,28},{16,32},{20,36},{24,40},{28,44},{32,4... | collective-permute-start | bytes 196616 | tf_op jit(solution)/shard_map/ppermute | solution.py:13
  156.9 25.3 %collective-permute-start.17 = (bf16[2,64,4,64]{3,1,2,0:T(8,128)(2,1)}, bf16[2,64,4,64]{3,1,2,0:T(8,128)(2,1)}, u32[]{:S(2)}, u32[]{:S(2)}) collective-permute-start(bf16[2,64,4,64]{3,1,2,0:T(8,128)(2,1)} %gather_fusion.2), channel_id=1, source_target_pairs={{0,20},{4,24},{8,28},{12,32},{16,36},{20,40},{24,44},{28,48},{32,5... | collective-permute-start | bytes 196616 | tf_op jit(solution)/shard_map/ppermute | solution.py:13
  158.4 29.3 %collective-permute-start.21 = (bf16[2,64,4,64]{3,1,2,0:T(8,128)(2,1)}, bf16[2,64,4,64]{3,1,2,0:T(8,128)(2,1)}, u32[]{:S(2)}, u32[]{:S(2)}) collective-permute-start(bf16[2,64,4,64]{3,1,2,0:T(8,128)(2,1)} %gather_fusion.2), channel_id=1, source_target_pairs={{0,24},{4,28},{8,32},{12,36},{16,40},{20,44},{24,48},{28,52},{32,5... | collective-permute-start | bytes 196616 | tf_op jit(solution)/shard_map/ppermute | solution.py:13
  170.2 10.7 %copy-start.22 = (bf16[2,128,1,256]{1,3,0,2:T(8,128)(2,1)S(1)}, bf16[2,128,1,256]{1,3,0,2:T(8,128)(2,1)}, u32[]{:S(2)}) copy-start(bf16[2,128,1,256]{1,3,0,2:T(8,128)(2,1)} %copy.183) | copy-start | bytes 393220
  170.9 18.4 %collective-permute-start.25 = (bf16[2,64,4,64]{3,1,2,0:T(8,128)(2,1)S(1)}, bf16[2,64,4,64]{3,1,2,0:T(8,128)(2,1)S(1)}, u32[]{:S(2)}, u32[]{:S(2)}) collective-permute-start(bf16[2,64,4,64]{3,1,2,0:T(8,128)(2,1)S(1)} %copy-done.31), channel_id=1, source_target_pairs={{0,28},{4,32},{8,36},{12,40},{16,44},{20,48},{24,52},{28,56},{32,6... | collective-permute-start | bytes 196616 | tf_op jit(solution)/shard_map/ppermute | solution.py:13
  171.1 14.2 %copy-start.15 = (bf16[2,128,1,256]{1,3,0,2:T(8,128)(2,1)S(1)}, bf16[2,128,1,256]{1,3,0,2:T(8,128)(2,1)}, u32[]{:S(2)}) copy-start(bf16[2,128,1,256]{1,3,0,2:T(8,128)(2,1)} %copy.189) | copy-start | bytes 393220
  172.3 14.2 %copy-start.21 = (bf16[2,128,1,256]{1,3,0,2:T(8,128)(2,1)S(1)}, bf16[2,128,1,256]{1,3,0,2:T(8,128)(2,1)}, u32[]{:S(2)}) copy-start(bf16[2,128,1,256]{1,3,0,2:T(8,128)(2,1)} %copy.188) | copy-start | bytes 393220
  172.9 20.0 %collective-permute-start.35 = (f32[2,4,64]{2,1,0:T(4,128)S(1)}, f32[2,4,64]{2,1,0:T(4,128)S(1)}, u32[]{:S(2)}, u32[]{:S(2)}) collective-permute-start(f32[2,4,64]{2,1,0:T(4,128)S(1)} %convert_reduce_fusion.8), channel_id=1, source_target_pairs={{0,248},{4,252},{8,0},{12,4},{16,8},{20,12},{24,16},{28,20},{32,24... | collective-permute-start | bytes 6152 | tf_op jit(solution)/shard_map/ppermute | solution.py:13
  175.0 12.8 %copy-start.14 = (bf16[2,128,1,256]{1,3,0,2:T(8,128)(2,1)S(1)}, bf16[2,128,1,256]{1,3,0,2:T(8,128)(2,1)}, u32[]{:S(2)}) copy-start(bf16[2,128,1,256]{1,3,0,2:T(8,128)(2,1)} %copy.194) | copy-start | bytes 393220
  176.5 15.8 %copy-start.13 = (bf16[2,128,1,256]{1,3,0,2:T(8,128)(2,1)S(1)}, bf16[2,128,1,256]{1,3,0,2:T(8,128)(2,1)}, u32[]{:S(2)}) copy-start(bf16[2,128,1,256]{1,3,0,2:T(8,128)(2,1)} %copy.199) | copy-start | bytes 393220
  176.8 16.7 %collective-permute-start.36 = (f32[2,4,64]{2,1,0:T(4,128)S(1)}, f32[2,4,64]{2,1,0:T(4,128)S(1)}, u32[]{:S(2)}, u32[]{:S(2)}) collective-permute-start(f32[2,4,64]{2,1,0:T(4,128)S(1)} %convert_reduce_fusion.7), channel_id=1, source_target_pairs={{0,244},{4,248},{8,252},{12,0},{16,4},{20,8},{24,12},{28,16},{32,2... | collective-permute-start | bytes 6152 | tf_op jit(solution)/shard_map/ppermute | solution.py:13
  180.9 21.5 %copy-start.20 = (bf16[2,128,1,256]{1,3,0,2:T(8,128)(2,1)S(1)}, bf16[2,128,1,256]{1,3,0,2:T(8,128)(2,1)}, u32[]{:S(2)}) copy-start(bf16[2,128,1,256]{1,3,0,2:T(8,128)(2,1)} %copy.193) | copy-start | bytes 393220
  181.9 27.9 %copy-start.19 = (bf16[2,128,1,256]{1,3,0,2:T(8,128)(2,1)S(1)}, bf16[2,128,1,256]{1,3,0,2:T(8,128)(2,1)}, u32[]{:S(2)}) copy-start(bf16[2,128,1,256]{1,3,0,2:T(8,128)(2,1)} %copy.198) | copy-start | bytes 393220
  182.2 15.5 %collective-permute-start.37 = (f32[2,4,64]{2,1,0:T(4,128)S(1)}, f32[2,4,64]{2,1,0:T(4,128)S(1)}, u32[]{:S(2)}, u32[]{:S(2)}) collective-permute-start(f32[2,4,64]{2,1,0:T(4,128)S(1)} %convert_reduce_fusion.6), channel_id=1, source_target_pairs={{0,240},{4,244},{8,248},{12,252},{16,0},{20,4},{24,8},{28,12},{32,... | collective-permute-start | bytes 6152 | tf_op jit(solution)/shard_map/ppermute | solution.py:13
  187.7 10.7 %collective-permute-start.38 = (f32[2,4,64]{2,1,0:T(4,128)S(1)}, f32[2,4,64]{2,1,0:T(4,128)S(1)}, u32[]{:S(2)}, u32[]{:S(2)}) collective-permute-start(f32[2,4,64]{2,1,0:T(4,128)S(1)} %convert_reduce_fusion.5), channel_id=1, source_target_pairs={{0,236},{4,240},{8,244},{12,248},{16,252},{20,0},{24,4},{28,8},{32... | collective-permute-start | bytes 6152 | tf_op jit(solution)/shard_map/ppermute | solution.py:13
  189.3 9.1 %collective-permute-start.39 = (f32[2,4,64]{2,1,0:T(4,128)S(1)}, f32[2,4,64]{2,1,0:T(4,128)S(1)}, u32[]{:S(2)}, u32[]{:S(2)}) collective-permute-start(f32[2,4,64]{2,1,0:T(4,128)S(1)} %convert_reduce_fusion.4), channel_id=1, source_target_pairs={{0,232},{4,236},{8,240},{12,244},{16,248},{20,252},{24,0},{28,4},{... | collective-permute-start | bytes 6152 | tf_op jit(solution)/shard_map/ppermute | solution.py:13
  192.9 11.3 %collective-permute-start.28 = (f32[2,4,64]{2,1,0:T(4,128)S(1)}, f32[2,4,64]{2,1,0:T(4,128)S(1)}, u32[]{:S(2)}, u32[]{:S(2)}) collective-permute-start(f32[2,4,64]{2,1,0:T(4,128)S(1)} %get-tuple-element.70), channel_id=1, source_target_pairs={{0,248},{4,252},{8,0},{12,4},{16,8},{20,12},{24,16},{28,20},{32,24... | collective-permute-start | bytes 6152 | tf_op jit(solution)/shard_map/ppermute | solution.py:13
  193.5 13.7 %collective-permute-start.29 = (f32[2,4,64]{2,1,0:T(4,128)S(1)}, f32[2,4,64]{2,1,0:T(4,128)S(1)}, u32[]{:S(2)}, u32[]{:S(2)}) collective-permute-start(f32[2,4,64]{2,1,0:T(4,128)S(1)} %get-tuple-element.72), channel_id=1, source_target_pairs={{0,244},{4,248},{8,252},{12,0},{16,4},{20,8},{24,12},{28,16},{32,2... | collective-permute-start | bytes 6152 | tf_op jit(solution)/shard_map/ppermute | solution.py:13
  197.7 9.6 %collective-permute-start.30 = (f32[2,4,64]{2,1,0:T(4,128)S(1)}, f32[2,4,64]{2,1,0:T(4,128)S(1)}, u32[]{:S(2)}, u32[]{:S(2)}) collective-permute-start(f32[2,4,64]{2,1,0:T(4,128)S(1)} %get-tuple-element.74), channel_id=1, source_target_pairs={{0,240},{4,244},{8,248},{12,252},{16,0},{20,4},{24,8},{28,12},{32,... | collective-permute-start | bytes 6152 | tf_op jit(solution)/shard_map/ppermute | solution.py:13
  198.5 10.2 %collective-permute-start.31 = (f32[2,4,64]{2,1,0:T(4,128)S(1)}, f32[2,4,64]{2,1,0:T(4,128)S(1)}, u32[]{:S(2)}, u32[]{:S(2)}) collective-permute-start(f32[2,4,64]{2,1,0:T(4,128)S(1)} %get-tuple-element.76), channel_id=1, source_target_pairs={{0,236},{4,240},{8,244},{12,248},{16,252},{20,0},{24,4},{28,8},{32... | collective-permute-start | bytes 6152 | tf_op jit(solution)/shard_map/ppermute | solution.py:13
  198.5 5.7 %collective-permute-start.40 = (f32[2,4,64]{2,1,0:T(4,128)S(1)}, f32[2,4,64]{2,1,0:T(4,128)S(1)}, u32[]{:S(2)}, u32[]{:S(2)}) collective-permute-start(f32[2,4,64]{2,1,0:T(4,128)S(1)} %convert_reduce_fusion.3), channel_id=1, source_target_pairs={{0,228},{4,232},{8,236},{12,240},{16,244},{20,248},{24,252},{28,0}... | collective-permute-start | bytes 6152 | tf_op jit(solution)/shard_map/ppermute | solution.py:13
  204.2 56.2 %collective-permute-start.1 = (bf16[8,64,4,64]{3,1,2,0:T(8,128)(2,1)}, bf16[8,64,4,64]{3,1,2,0:T(8,128)(2,1)}, u32[]{:S(2)}, u32[]{:S(2)}) collective-permute-start(bf16[8,64,4,64]{3,1,2,0:T(8,128)(2,1)} %copy.159), channel_id=1, source_target_pairs={{0,4},{4,8},{8,12},{12,16},{16,20},{20,24},{24,28},{28,32},{32,36}... | collective-permute-start | bytes 786440 | tf_op jit(solution)/shard_map/ppermute | solution.py:13
  204.2 6.7 %collective-permute-start.32 = (f32[2,4,64]{2,1,0:T(4,128)S(1)}, f32[2,4,64]{2,1,0:T(4,128)S(1)}, u32[]{:S(2)}, u32[]{:S(2)}) collective-permute-start(f32[2,4,64]{2,1,0:T(4,128)S(1)} %get-tuple-element.78), channel_id=1, source_target_pairs={{0,232},{4,236},{8,240},{12,244},{16,248},{20,252},{24,0},{28,4},{... | collective-permute-start | bytes 6152 | tf_op jit(solution)/shard_map/ppermute | solution.py:13
  207.3 5.9 %collective-permute-start.33 = (f32[2,4,64]{2,1,0:T(4,128)S(1)}, f32[2,4,64]{2,1,0:T(4,128)S(1)}, u32[]{:S(2)}, u32[]{:S(2)}) collective-permute-start(f32[2,4,64]{2,1,0:T(4,128)S(1)} %get-tuple-element.80), channel_id=1, source_target_pairs={{0,228},{4,232},{8,236},{12,240},{16,244},{20,248},{24,252},{28,0}... | collective-permute-start | bytes 6152 | tf_op jit(solution)/shard_map/ppermute | solution.py:13
  207.3 11.0 %collective-permute-start.6 = (f32[2,64,4,64]{1,3,2,0:T(8,128)S(1)}, f32[2,64,4,64]{1,3,2,0:T(8,128)S(1)}, u32[]{:S(2)}, u32[]{:S(2)}) collective-permute-start(f32[2,64,4,64]{1,3,2,0:T(8,128)S(1)} %convolution_bitcast_fusion.8), channel_id=1, source_target_pairs={{0,248},{4,252},{8,0},{12,4},{16,8},{20,12},{24,16},{28,20},{32,24... | collective-permute-start | bytes 393224 | tf_op jit(solution)/shard_map/ppermute | solution.py:13
  208.6 14.4 %collective-permute-start.10 = (f32[2,64,4,64]{1,3,2,0:T(8,128)S(1)}, f32[2,64,4,64]{1,3,2,0:T(8,128)S(1)}, u32[]{:S(2)}, u32[]{:S(2)}) collective-permute-start(f32[2,64,4,64]{1,3,2,0:T(8,128)S(1)} %convolution_bitcast_fusion.7), channel_id=1, source_target_pairs={{0,244},{4,248},{8,252},{12,0},{16,4},{20,8},{24,12},{28,16},{32,2... | collective-permute-start | bytes 393224 | tf_op jit(solution)/shard_map/ppermute | solution.py:13
  210.9 30.3 %collective-permute-start.14 = (f32[2,64,4,64]{1,3,2,0:T(8,128)}, f32[2,64,4,64]{1,3,2,0:T(8,128)}, u32[]{:S(2)}, u32[]{:S(2)}) collective-permute-start(f32[2,64,4,64]{1,3,2,0:T(8,128)} %convolution_bitcast_fusion.6), channel_id=1, source_target_pairs={{0,240},{4,244},{8,248},{12,252},{16,0},{20,4},{24,8},{28,12},{32,... | collective-permute-start | bytes 393224 | tf_op jit(solution)/shard_map/ppermute | solution.py:13
  213.1 32.8 %collective-permute-start.18 = (f32[2,64,4,64]{1,3,2,0:T(8,128)}, f32[2,64,4,64]{1,3,2,0:T(8,128)}, u32[]{:S(2)}, u32[]{:S(2)}) collective-permute-start(f32[2,64,4,64]{1,3,2,0:T(8,128)} %convolution_bitcast_fusion.5), channel_id=1, source_target_pairs={{0,236},{4,240},{8,244},{12,248},{16,252},{20,0},{24,4},{28,8},{32... | collective-permute-start | bytes 393224 | tf_op jit(solution)/shard_map/ppermute | solution.py:13
  218.3 32.5 %collective-permute-start.22 = (f32[2,64,4,64]{1,3,2,0:T(8,128)}, f32[2,64,4,64]{1,3,2,0:T(8,128)}, u32[]{:S(2)}, u32[]{:S(2)}) collective-permute-start(f32[2,64,4,64]{1,3,2,0:T(8,128)} %convolution_bitcast_fusion.4), channel_id=1, source_target_pairs={{0,232},{4,236},{8,240},{12,244},{16,248},{20,252},{24,0},{28,4},{... | collective-permute-start | bytes 393224 | tf_op jit(solution)/shard_map/ppermute | solution.py:13
  223.8 31.8 %collective-permute-start.26 = (f32[2,64,4,64]{1,3,2,0:T(8,128)}, f32[2,64,4,64]{1,3,2,0:T(8,128)}, u32[]{:S(2)}, u32[]{:S(2)}) collective-permute-start(f32[2,64,4,64]{1,3,2,0:T(8,128)} %convolution_bitcast_fusion.3), channel_id=1, source_target_pairs={{0,228},{4,232},{8,236},{12,240},{16,244},{20,248},{24,252},{28,0}... | collective-permute-start | bytes 393224 | tf_op jit(solution)/shard_map/ppermute | solution.py:13
  262.1 10.6 %copy-start.39 = (f32[8,4,64]{2,1,0:T(4,128)S(1)}, f32[8,4,64]{2,1,0:T(4,128)}, u32[]{:S(2)}) copy-start(f32[8,4,64]{2,1,0:T(4,128)} %copy-done.38) | copy-start | bytes 24580
  262.2 11.2 %copy-start.41 = (f32[8,4,64]{2,1,0:T(4,128)S(1)}, f32[8,4,64]{2,1,0:T(4,128)}, u32[]{:S(2)}) copy-start(f32[8,4,64]{2,1,0:T(4,128)} %copy-done.40) | copy-start | bytes 24580
  262.2 11.8 %copy-start.43 = (f32[8,4,64]{2,1,0:T(4,128)S(1)}, f32[8,4,64]{2,1,0:T(4,128)}, u32[]{:S(2)}) copy-start(f32[8,4,64]{2,1,0:T(4,128)} %copy-done.42) | copy-start | bytes 24580
  262.2 12.4 %copy-start.30 = (f32[9,8,4,64]{3,2,1,0:T(4,128)S(1)}, f32[9,8,4,64]{3,2,1,0:T(4,128)}, u32[]{:S(2)}) copy-start(f32[9,8,4,64]{3,2,1,0:T(4,128)} %constant_dynamic-update-slice_fusion.7) | copy-start | bytes 221188
  262.2 12.4 %collective-permute-start.27 = (f32[8,4,64]{2,1,0:T(4,128)S(1)}, f32[8,4,64]{2,1,0:T(4,128)S(1)}, u32[]{:S(2)}, u32[]{:S(2)}) collective-permute-start(f32[8,4,64]{2,1,0:T(4,128)S(1)} %get-tuple-element.68), channel_id=1, source_target_pairs={{0,252},{4,0},{8,4},{12,8},{16,12},{20,16},{24,20},{28,24},{32,28}... | collective-permute-start | bytes 24584 | tf_op jit(solution)/shard_map/ppermute | solution.py:13
  264.0 6.4 %collective-permute-start.34 = (f32[8,4,64]{2,1,0:T(4,128)S(1)}, f32[8,4,64]{2,1,0:T(4,128)S(1)}, u32[]{:S(2)}, u32[]{:S(2)}) collective-permute-start(f32[8,4,64]{2,1,0:T(4,128)S(1)} %convert_reduce_fusion), channel_id=1, source_target_pairs={{0,252},{4,0},{8,4},{12,8},{16,12},{20,16},{24,20},{28,24},{32,28}... | collective-permute-start | bytes 24584 | tf_op jit(solution)/shard_map/ppermute | solution.py:13
  265.7 18.1 %copy-start.2 = (f32[8,64,4,64]{1,3,2,0:T(8,128)S(1)}, f32[8,64,4,64]{1,3,2,0:T(8,128)}, u32[]{:S(2)}) copy-start(f32[8,64,4,64]{1,3,2,0:T(8,128)} %copy.176) | copy-start | bytes 1572868
  265.7 17.0 %collective-permute-start.2 = (f32[8,64,4,64]{1,3,2,0:T(8,128)S(1)}, f32[8,64,4,64]{1,3,2,0:T(8,128)S(1)}, u32[]{:S(2)}, u32[]{:S(2)}) collective-permute-start(f32[8,64,4,64]{1,3,2,0:T(8,128)S(1)} %convolution_bitcast_fusion), channel_id=1, source_target_pairs={{0,252},{4,0},{8,4},{12,8},{16,12},{20,16},{24,20},{28,24},{32,28}... | collective-permute-start | bytes 1572872 | tf_op jit(solution)/shard_map/ppermute | solution.py:13
  297.6 69.8 %copy-start.8 = (bf16[512,1024]{1,0:T(8,128)(2,1)S(1)}, bf16[512,1024]{1,0:T(8,128)(2,1)}, u32[]{:S(2)}) copy-start(bf16[512,1024]{1,0:T(8,128)(2,1)} %all-gather.2.cloned.1.call-done) | copy-start | bytes 3145732
  300.6 69.0 %copy-start.45 = (f32[1024]{0:T(1024)S(1)}, f32[1024]{0:T(1024)}, u32[]{:S(2)}) copy-start(f32[1024]{0:T(1024)} %param.15) | copy-start | bytes 12292
  300.6 105.7 %reduce-scatter.2.cloned.1.call-start = ((), (), s32[]{:S(2)}) async-start(), calls=%async_computation.3 | async-start | bytes 1310720 | tf_op jit(solution)/shard_map/reduce_scatter | solution.py:168
  371.1 10.2 %copy-start.47 = (s32[8]{0:T(128)S(1)}, s32[8]{0:T(128)}, u32[]{:S(2)}) copy-start(s32[8]{0:T(128)} %param.23) | copy-start | bytes 100
  380.2 26.1 %copy-start.9 = (bf16[512,1024]{1,0:T(8,128)(2,1)S(1)}, bf16[512,1024]{1,0:T(8,128)(2,1)}, u32[]{:S(2)}) copy-start(bf16[512,1024]{1,0:T(8,128)(2,1)} %multiply_convert_fusion) | copy-start | bytes 3145732
  (28 other events, 130.0 us)
Sparse Core Ops, SparseCore 0:
  17.5 30.9 all-gather.1
  300.7 66.6 all-reduce.2
  380.4 25.8 reduce-scatter.1
where the time goes:
time: 430 us; the launch traced here: 425 us
  waiting for transfers between devices  105 us (24%)
  local copies, waits for them, and re-layouts  102 us (24%)
  matrix products  102 us (24%)
  starting transfers between devices  72.5 us (17%)
  other arithmetic  19.6 us (5%)
  between operations  15.3 us (4%)
  blocking collectives  8.47 us (2%)
    ppermute x41, starting transfers between devices, from_behind(): lax.ppermute(value, axis, [(i, (i + by) % size) for i in range(size)])  72.2 us
    psum x1, waiting for transfers between devices, shards(): summed = lax.psum(branch, 'tp')  66.8 us
    dot_general x8, matrix products, page_rows(): jnp.einsum('rs,spcf->rpcf', picker, cache_pool, preferred_element_type=jn...  64.3 us
    reduce_scatter x1, waiting for transfers between devices, shards(): lax.psum_scatter(jnp.dot(inner, w_down, preferred_element_type=jnp.float3...  22.1 us
    slice x16, local copies, waits for them, and re-layouts, rows_split(): rows[:, :, 0].reshape(requests, page_len, heads_local, HD)  19.2 us
    scatter x12, local copies, waits for them, and re-layouts, spread_back(): jnp.zeros((requests,) + arrived[0].shape[1:], jnp.float32).at[long_ids]  17.2 us
    ppermute x41, waiting for transfers between devices, from_behind(): lax.ppermute(value, axis, [(i, (i + by) % size) for i in range(size)])  16.4 us
    unnamed x119, local copies, waits for them, and re-layouts  14.9 us
  transfers between devices with their start and end apart: 44, of which 6 were waited for; matrix products, arithmetic and copies ran while one was open for 42% of the time, Pallas kernels for 0%

commit v1 on v0

--- a/solution.py
+++ b/solution.py
@@ -157,7 +157,7 @@
     )
     branch = jnp.dot(attended, w_out, preferred_element_type=jnp.float32)
     second_share = lax.dynamic_slice_in_dim(second_gain, start, share, 0)
-    summed = lax.psum(branch, "tp")
+    summed = jnp.sum(lax.all_gather(branch, "tp"), axis=0)
     mixed_all = gathered.astype(jnp.float32) + summed
     whole_sums = (jnp.sum(mixed_all, axis=-1), jnp.sum(mixed_all * mixed_all, axis=-1))
     normed_all = norm_from_sums(mixed_all, whole_sums, first_gain, width_all).astype(jnp.bfloat16)

time: 430 us -> 458 us (1.065)
  waiting for transfers between devices: 105 us -> 128 us
  other arithmetic: 19.6 us -> 25.6 us
    all_gather x0 -> x1, waiting for transfers between devices: none -> 88.6 us  [shards(): summed = jnp.sum(lax.all_gather(branch, 'tp'), axis=0)]
    psum x1 -> x0, waiting for transfers between devices: 66.8 us -> none  [shards(): summed = lax.psum(branch, 'tp')]
    reduce_sum x0 -> x1, other arithmetic: none -> 5.99 us  [shards(): summed = jnp.sum(lax.all_gather(branch, 'tp'), axis=0)]
  transfers between devices with their start and end apart: 44 -> 44, of which waited for: 6 -> 6; matrix products, arithmetic and copies ran while one was open for 42% -> 39% of each run, Pallas kernels for 0% -> 0%
where the time goes in v1:
time: 458 us; the launch traced here: 453 us
  waiting for transfers between devices  128 us (28%)
  matrix products  102 us (22%)
  local copies, waits for them, and re-layouts  101 us (22%)
  starting transfers between devices  72.5 us (16%)
  other arithmetic  25.6 us (6%)
  between operations  15.3 us (3%)
  blocking collectives  8.47 us (2%)
    all_gather x1, waiting for transfers between devices, shards(): summed = jnp.sum(lax.all_gather(branch, 'tp'), axis=0)  88.6 us
    ppermute x41, starting transfers between devices, from_behind(): lax.ppermute(value, axis, [(i, (i + by) % size) for i in range(size)])  72.2 us
    dot_general x8, matrix products, page_rows(): jnp.einsum('rs,spcf->rpcf', picker, cache_pool, preferred_element_type=jn...  64.3 us
    reduce_scatter x1, waiting for transfers between devices, shards(): lax.psum_scatter(jnp.dot(inner, w_down, preferred_element_type=jnp.float3...  23.2 us
    slice x16, local copies, waits for them, and re-layouts, rows_split(): rows[:, :, 0].reshape(requests, page_len, heads_local, HD)  19.1 us
    scatter x12, local copies, waits for them, and re-layouts, spread_back(): jnp.zeros((requests,) + arrived[0].shape[1:], jnp.float32).at[long_ids]  17.2 us
    ppermute x41, waiting for transfers between devices, from_behind(): lax.ppermute(value, axis, [(i, (i + by) % size) for i in range(size)])  16.4 us
    unnamed x119, local copies, waits for them, and re-layouts  14.9 us
  transfers between devices with their start and end apart: 44, of which 6 were waited for; matrix products, arithmetic and copies ran while one was open for 39% of the time, Pallas kernels for 0%

profile of v1, /device:TPU:2, one launch (start us, length us, event | category | flops | bytes accessed | tf_op | source)
XLA Modules:
  0.0 452.9 jit_solution(8334085113621228535)
XLA Ops:
  11.1 4.3 collective-permute-start.15
  21.2 7.9 %convolution_convert_fusion.2 = bf16[8,128,2,256]{3,0,2,1:T(8,128)(2,1)S(1)} fusion(bf16[64,128,2,256]{3,2,1,0:T(2,128)(2,1)} %param.19, s32[8]{0:T(128)S(1)} %get-tuple-element.46), kind=kOutput, calls=%fused_computation.56 | convolution fusion | flops 67633664 | bytes 9437216 | tf_op jit(solution)/shard_map/rs,spcf->rpcf/dot_general | solution.py:46
  31.6 2.3 copy.165
  33.9 8.4 %convolution_convert_fusion.1 = bf16[8,128,2,256]{3,0,2,1:T(8,128)(2,1)S(1)} fusion(bf16[64,128,2,256]{3,2,1,0:T(2,128)(2,1)} %param.19, s32[8]{0:T(128)S(1)} %get-tuple-element.45), kind=kOutput, calls=%fused_computation.55 | convolution fusion | flops 67633664 | bytes 9437216 | tf_op jit(solution)/shard_map/rs,spcf->rpcf/dot_general | solution.py:46
  43.3 2.2 copy.168
  45.5 2.2 copy.170
  51.3 2.9 collective-permute-start.19
  55.3 8.0 %fusion.26 = bf16[2,128,2,256]{3,0,2,1:T(2,128)(2,1)S(1)} fusion(bf16[64,128,2,256]{3,2,1,0:T(2,128)(2,1)} %param.19, s32[2]{0:T(128)S(1)} %gather_fusion), kind=kOutput, calls=%fused_computation.77 | convolution fusion | flops 16908416 | bytes 8650760 | tf_op jit(solution)/shard_map/rs,spcf->rpcf/dot_general | solution.py:46
  64.8 8.0 %fusion.29 = bf16[2,128,2,256]{3,0,2,1:T(2,128)(2,1)S(1)} fusion(bf16[64,128,2,256]{3,2,1,0:T(2,128)(2,1)} %param.19, s32[2]{0:T(128)S(1)} %gather_fusion.3), kind=kOutput, calls=%fused_computation.78 | convolution fusion | flops 16908416 | bytes 8650760 | tf_op jit(solution)/shard_map/rs,spcf->rpcf/dot_general | solution.py:46
  73.6 2.4 collective-permute-start.4
  76.1 3.1 collective-permute-start.8
  79.9 8.0 %fusion.32 = bf16[2,128,2,256]{3,0,2,1:T(2,128)(2,1)S(1)} fusion(bf16[64,128,2,256]{3,2,1,0:T(2,128)(2,1)} %param.19, s32[2]{0:T(128)S(1)} %gather_fusion.5), kind=kOutput, calls=%fused_computation.79 | convolution fusion | flops 16908416 | bytes 8650760 | tf_op jit(solution)/shard_map/rs,spcf->rpcf/dot_general | solution.py:46
  89.4 8.0 %fusion.35 = bf16[2,128,2,256]{3,0,2,1:T(2,128)(2,1)S(1)} fusion(bf16[64,128,2,256]{3,2,1,0:T(2,128)(2,1)} %param.19, s32[2]{0:T(128)S(1)} %gather_fusion.7), kind=kOutput, calls=%fused_computation.80 | convolution fusion | flops 16908416 | bytes 8650760 | tf_op jit(solution)/shard_map/rs,spcf->rpcf/dot_general | solution.py:46
  98.3 2.0 collective-permute-start.12
  100.3 3.7 collective-permute-start.16
  104.7 8.0 %fusion.38 = bf16[2,128,2,256]{3,0,2,1:T(2,128)(2,1)S(1)} fusion(bf16[64,128,2,256]{3,2,1,0:T(2,128)(2,1)} %param.19, s32[2]{0:T(128)S(1)} %gather_fusion.9), kind=kOutput, calls=%fused_computation.81 | convolution fusion | flops 16908416 | bytes 8650760 | tf_op jit(solution)/shard_map/rs,spcf->rpcf/dot_general | solution.py:46
  114.2 8.0 %fusion.41 = bf16[2,128,2,256]{3,0,2,1:T(2,128)(2,1)S(1)} fusion(bf16[64,128,2,256]{3,2,1,0:T(2,128)(2,1)} %param.19, s32[2]{0:T(128)S(1)} %gather_fusion.11), kind=kOutput, calls=%fused_computation.82 | convolution fusion | flops 16908416 | bytes 8650760 | tf_op jit(solution)/shard_map/rs,spcf->rpcf/dot_general | solution.py:46
  124.7 1.7 copy.178
  127.1 1.7 copy.183
  128.8 1.7 copy.184
  130.5 1.7 copy.188
  132.1 1.7 copy.189
  133.8 1.7 copy.193
  135.5 1.7 copy.194
  138.7 1.8 collective-permute-start.24
  140.6 3.8 collective-permute-done.20
  144.5 2.7 fusion.45
  150.9 2.3 gather_fusion.2
  154.7 2.2 collective-permute-start.13
  159.1 2.0 convert_element_type.221
  161.1 2.0 convert_element_type.227
  172.8 2.1 collective-permute-start.35
  176.7 2.9 collective-permute-start.36
  182.1 3.0 collective-permute-start.37
  189.2 3.0 collective-permute-start.39
  193.5 4.2 collective-permute-start.29
  198.4 4.0 collective-permute-start.40
  204.1 3.1 collective-permute-start.32
  210.8 2.2 collective-permute-start.14
  213.3 4.9 %collective-permute-done.6 = f32[2,64,4,64]{1,3,2,0:T(8,128)S(1)} collective-permute-done((f32[2,64,4,64]{1,3,2,0:T(8,128)S(1)}, f32[2,64,4,64]{1,3,2,0:T(8,128)S(1)}, u32[]{:S(2)}, u32[]{:S(2)}) %collective-permute-start.6) | collective-permute-done | bytes 131104 | tf_op jit(solution)/shard_map/ppermute | solution.py:13
  218.2 4.8 %collective-permute-start.22 = (f32[2,64,4,64]{1,3,2,0:T(8,128)}, f32[2,64,4,64]{1,3,2,0:T(8,128)}, u32[]{:S(2)}, u32[]{:S(2)}) collective-permute-start(f32[2,64,4,64]{1,3,2,0:T(8,128)} %convolution_bitcast_fusion.4), channel_id=1, source_target_pairs={{0,232},{4,236},{8,240},{12,244},{16,248},{20,252},{24,0},{28,4},{... | collective-permute-start | bytes 393224 | tf_op jit(solution)/shard_map/ppermute | solution.py:13
  233.5 1.5 scatter_fusion
  236.3 1.8 copy.180
  238.2 1.5 scatter_fusion.1
  241.1 1.8 copy.185
  243.0 1.5 scatter_fusion.2
  245.9 1.8 copy.190
  247.8 1.5 scatter_fusion.3
  250.7 1.8 copy.195
  252.6 1.5 scatter_fusion.4
  255.5 1.8 copy.200
  257.4 1.5 scatter_fusion.5
  260.3 1.8 select_reduce_fusion
  265.6 4.7 %collective-permute-start.2 = (f32[8,64,4,64]{1,3,2,0:T(8,128)S(1)}, f32[8,64,4,64]{1,3,2,0:T(8,128)S(1)}, u32[]{:S(2)}, u32[]{:S(2)}) collective-permute-start(f32[8,64,4,64]{1,3,2,0:T(8,128)S(1)} %convolution_bitcast_fusion), channel_id=1, source_target_pairs={{0,252},{4,0},{8,4},{12,8},{16,12},{20,16},{24,20},{28,24},{32,28}... | collective-permute-start | bytes 1572872 | tf_op jit(solution)/shard_map/ppermute | solution.py:13
  275.6 7.0 %collective-permute-done.2 = f32[8,64,4,64]{1,3,2,0:T(8,128)S(1)} collective-permute-done((f32[8,64,4,64]{1,3,2,0:T(8,128)S(1)}, f32[8,64,4,64]{1,3,2,0:T(8,128)S(1)}, u32[]{:S(2)}, u32[]{:S(2)}) %collective-permute-start.2) | collective-permute-done | bytes 524320 | tf_op jit(solution)/shard_map/ppermute | solution.py:13
  290.4 5.6 %multiply_reduce_fusion = f32[8,64,4,64]{1,3,2,0:T(8,128)S(1)} fusion(f32[9,8,64,4,64]{2,4,3,1,0:T(8,128)} %bitcast_dynamic-update-slice_fusion, f32[9,8,64,4]{2,3,1,0:T(4,128)S(1)} %get-tuple-element.21), kind=kLoop, calls=%fused_computation.31 | loop fusion | flops 2228224 | bytes 5316608 | tf_op jit(solution)/shard_map/reduce_sum | solution.py:29
  296.8 2.9 fusion.186
  299.7 88.6 %all-gather.6.cloned.1.call-done = f32[2048,1024]{1,0:T(8,128)} async-done(((f32[512,1024]{1,0:T(8,128)}), f32[2048,1024]{1,0:T(8,128)}) %all-gather.6.cloned.1.call-update) | async-done | bytes 8388624 | tf_op jit(solution)/shard_map/all_gather | solution.py:160
  388.4 6.0 %reduce_sum.164 = f32[512,1024]{1,0:T(8,128)} reduce(f32[4,512,1024]{2,1,0:T(8,128)} %bitcast.234, f32[]{:T(128)} %constant.54.clone.1), dimensions={0}, to_apply=%region_39.40 | reduce | flops 1572864 | bytes 10485764 | tf_op jit(solution)/shard_map/reduce_sum | solution.py:160
  394.3 2.2 fusion.77
  398.0 9.2 %convolution_convert_fusion = bf16[512,1024]{1,0:T(8,128)(2,1)} fusion(bf16[1024,1024]{1,0:T(8,128)(2,1)S(1)} %copy-done, bf16[512,1024]{1,0:T(8,128)(2,1)} %multiply_convert_fusion, bf16[1024,1024]{1,0:T(8,128)(2,1)} %param.16), kind=kOutput, calls=%fused_computation.54 | convolution fusion | flops 2182086656 | bytes 6291456 | tf_op jit(solution)/shard_map/dot_general | solution.py:169
  411.2 23.2 %reduce-scatter.2.cloned.1.call-done = bf16[512,256]{1,0:T(8,128)(2,1)} async-done(((bf16[512,1024]{1,0:T(8,128)(2,1)}), bf16[512,256]{1,0:T(8,128)(2,1)}) %reduce-scatter.2.cloned.1.call-update) | async-done | bytes 262160 | tf_op jit(solution)/shard_map/reduce_scatter | solution.py:168
  435.6 8.5 %all-reduce = (f32[512]{0:T(512)S(1)}, f32[512]{0:T(512)S(1)}) all-reduce(f32[512]{0:T(512)S(1)} %get-tuple-element.17, f32[512]{0:T(512)S(1)} %get-tuple-element.16), channel_id=1, replica_groups=mesh['req'=64,'tp'=4] {'tp'}, use_global_device_ids=true, to_apply=%region_46.47 | all-reduce | flops 1024 | bytes 8192 | tf_op jit(solution)/shard_map/psum | solution.py:175
  444.1 1.9 multiply_convert_fusion.1
  (339 shorter events, 105.9 us)
Async XLA Ops:
  7.2 390.8 %copy-start = (bf16[1024,1024]{1,0:T(8,128)(2,1)S(1)}, bf16[1024,1024]{1,0:T(8,128)(2,1)}, u32[]{:S(2)}) copy-start(bf16[1024,1024]{1,0:T(8,128)(2,1)} %param.17) | copy-start | bytes 6291460
  7.2 137.3 %all-gather.4.cloned.1.call-start = ((), (), s32[]{:S(2)}) async-start(), calls=%async_computation.1 | async-start | bytes 1310720 | tf_op jit(solution)/shard_map/all_gather | solution.py:102
  9.0 42.3 %collective-permute-start.7 = (bf16[2]{0:T(256)(128)(2,1)S(1)}, bf16[2]{0:T(256)(128)(2,1)S(1)}, u32[]{:S(2)}, u32[]{:S(2)}) collective-permute-start(bf16[2]{0:T(256)(128)(2,1)S(1)} %get-tuple-element.60), channel_id=1, source_target_pairs={{0,12},{4,16},{8,20},{12,24},{16,28},{20,32},{24,36},{28,40},{32,4... | collective-permute-start | bytes 20 | tf_op jit(solution)/shard_map/ppermute | solution.py:13
  9.9 44.2 %collective-permute-start.3 = (bf16[2]{0:T(256)(128)(2,1)S(1)}, bf16[2]{0:T(256)(128)(2,1)S(1)}, u32[]{:S(2)}, u32[]{:S(2)}) collective-permute-start(bf16[2]{0:T(256)(128)(2,1)S(1)} %get-tuple-element.60), channel_id=1, source_target_pairs={{0,8},{4,12},{8,16},{12,20},{16,24},{20,28},{24,32},{28,36},{32,40... | collective-permute-start | bytes 20 | tf_op jit(solution)/shard_map/ppermute | solution.py:13
  11.1 62.5 %collective-permute-start.15 = (bf16[2]{0:T(256)(128)(2,1)S(1)}, bf16[2]{0:T(256)(128)(2,1)S(1)}, u32[]{:S(2)}, u32[]{:S(2)}) collective-permute-start(bf16[2]{0:T(256)(128)(2,1)S(1)} %get-tuple-element.60), channel_id=1, source_target_pairs={{0,20},{4,24},{8,28},{12,32},{16,36},{20,40},{24,44},{28,48},{32,5... | collective-permute-start | bytes 20 | tf_op jit(solution)/shard_map/ppermute | solution.py:13
  15.4 60.7 %collective-permute-start.11 = (bf16[2]{0:T(256)(128)(2,1)S(1)}, bf16[2]{0:T(256)(128)(2,1)S(1)}, u32[]{:S(2)}, u32[]{:S(2)}) collective-permute-start(bf16[2]{0:T(256)(128)(2,1)S(1)} %get-tuple-element.60), channel_id=1, source_target_pairs={{0,16},{4,20},{8,24},{12,28},{16,32},{20,36},{24,40},{28,44},{32,4... | collective-permute-start | bytes 20 | tf_op jit(solution)/shard_map/ppermute | solution.py:13
  16.7 81.6 %collective-permute-start.23 = (bf16[2]{0:T(256)(128)(2,1)S(1)}, bf16[2]{0:T(256)(128)(2,1)S(1)}, u32[]{:S(2)}, u32[]{:S(2)}) collective-permute-start(bf16[2]{0:T(256)(128)(2,1)S(1)} %get-tuple-element.60), channel_id=1, source_target_pairs={{0,28},{4,32},{8,36},{12,40},{16,44},{20,48},{24,52},{28,56},{32,6... | collective-permute-start | bytes 20 | tf_op jit(solution)/shard_map/ppermute | solution.py:13
  17.4 371.0 %all-gather.6.cloned.1.call-start = ((), (), s32[]{:S(2)}) async-start(), calls=%async_computation.3 | async-start | bytes 10485760 | tf_op jit(solution)/shard_map/all_gather | solution.py:160
  51.3 49.1 %collective-permute-start.19 = (bf16[2]{0:T(256)(128)(2,1)S(1)}, bf16[2]{0:T(256)(128)(2,1)S(1)}, u32[]{:S(2)}, u32[]{:S(2)}) collective-permute-start(bf16[2]{0:T(256)(128)(2,1)S(1)} %get-tuple-element.60), channel_id=1, source_target_pairs={{0,24},{4,28},{8,32},{12,36},{16,40},{20,44},{24,48},{28,52},{32,5... | collective-permute-start | bytes 20 | tf_op jit(solution)/shard_map/ppermute | solution.py:13
  54.2 90.2 %collective-permute-start = (bf16[8,128]{1,0:T(8,128)(2,1)S(1)}, bf16[8,128]{1,0:T(8,128)(2,1)S(1)}, u32[]{:S(2)}, u32[]{:S(2)}) collective-permute-start(bf16[8,128]{1,0:T(8,128)(2,1)S(1)} %get-tuple-element.53), channel_id=1, source_target_pairs={{0,4},{4,8},{8,12},{12,16},{16,20},{20,24},{24,28},{28,32},{32,36}... | collective-permute-start | bytes 6152 | tf_op jit(solution)/shard_map/ppermute | solution.py:13
  73.6 65.1 %collective-permute-start.4 = (bf16[2,128]{1,0:T(2,128)(2,1)S(1)}, bf16[2,128]{1,0:T(2,128)(2,1)S(1)}, u32[]{:S(2)}, u32[]{:S(2)}) collective-permute-start(bf16[2,128]{1,0:T(2,128)(2,1)S(1)} %convert_element_type.237), channel_id=1, source_target_pairs={{0,8},{4,12},{8,16},{12,20},{16,24},{20,28},{24,32},{28,36},{32,40... | collective-permute-start | bytes 1544 | tf_op jit(solution)/shard_map/ppermute | solution.py:13
  76.1 62.7 %collective-permute-start.8 = (bf16[2,128]{1,0:T(2,128)(2,1)S(1)}, bf16[2,128]{1,0:T(2,128)(2,1)S(1)}, u32[]{:S(2)}, u32[]{:S(2)}) collective-permute-start(bf16[2,128]{1,0:T(2,128)(2,1)S(1)} %convert_element_type.241), channel_id=1, source_target_pairs={{0,12},{4,16},{8,20},{12,24},{16,28},{20,32},{24,36},{28,40},{32,4... | collective-permute-start | bytes 1544 | tf_op jit(solution)/shard_map/ppermute | solution.py:13
  98.3 42.3 %collective-permute-start.12 = (bf16[2,128]{1,0:T(2,128)(2,1)S(1)}, bf16[2,128]{1,0:T(2,128)(2,1)S(1)}, u32[]{:S(2)}, u32[]{:S(2)}) collective-permute-start(bf16[2,128]{1,0:T(2,128)(2,1)S(1)} %convert_element_type.245), channel_id=1, source_target_pairs={{0,16},{4,20},{8,24},{12,28},{16,32},{20,36},{24,40},{28,44},{32,4... | collective-permute-start | bytes 1544 | tf_op jit(solution)/shard_map/ppermute | solution.py:13
  100.3 40.3 %collective-permute-start.16 = (bf16[2,128]{1,0:T(2,128)(2,1)S(1)}, bf16[2,128]{1,0:T(2,128)(2,1)S(1)}, u32[]{:S(2)}, u32[]{:S(2)}) collective-permute-start(bf16[2,128]{1,0:T(2,128)(2,1)S(1)} %convert_element_type.249), channel_id=1, source_target_pairs={{0,20},{4,24},{8,28},{12,32},{16,36},{20,40},{24,44},{28,48},{32,5... | collective-permute-start | bytes 1544 | tf_op jit(solution)/shard_map/ppermute | solution.py:13
  114.2 12.2 %copy-start.26 = (bf16[2,128,1,256]{3,0,2,1:T(2,128)(2,1)S(1)}, bf16[2,128,1,256]{3,0,2,1:T(2,128)(2,1)}, u32[]{:S(2)}) copy-start(bf16[2,128,1,256]{3,0,2,1:T(2,128)(2,1)} %get-tuple-element.36) | copy-start | bytes 393220
  123.9 14.1 %copy-start.27 = (bf16[2,128,1,256]{3,0,2,1:T(2,128)(2,1)S(1)}, bf16[2,128,1,256]{3,0,2,1:T(2,128)(2,1)}, u32[]{:S(2)}) copy-start(bf16[2,128,1,256]{3,0,2,1:T(2,128)(2,1)} %get-tuple-element.28) | copy-start | bytes 393220
  124.7 12.5 %copy-start.28 = (bf16[2,128,1,256]{3,0,2,1:T(2,128)(2,1)S(1)}, bf16[2,128,1,256]{3,0,2,1:T(2,128)(2,1)}, u32[]{:S(2)}) copy-start(bf16[2,128,1,256]{3,0,2,1:T(2,128)(2,1)} %get-tuple-element.29) | copy-start | bytes 393220
  138.7 5.7 %collective-permute-start.20 = (bf16[2,128]{1,0:T(2,128)(2,1)S(1)}, bf16[2,128]{1,0:T(2,128)(2,1)S(1)}, u32[]{:S(2)}, u32[]{:S(2)}) collective-permute-start(bf16[2,128]{1,0:T(2,128)(2,1)S(1)} %convert_element_type.253), channel_id=1, source_target_pairs={{0,24},{4,28},{8,32},{12,36},{16,40},{20,44},{24,48},{28,52},{32,5... | collective-permute-start | bytes 1544 | tf_op jit(solution)/shard_map/ppermute | solution.py:13
  138.7 5.6 %collective-permute-start.24 = (bf16[2,128]{1,0:T(2,128)(2,1)S(1)}, bf16[2,128]{1,0:T(2,128)(2,1)S(1)}, u32[]{:S(2)}, u32[]{:S(2)}) collective-permute-start(bf16[2,128]{1,0:T(2,128)(2,1)S(1)} %convert_element_type.257), channel_id=1, source_target_pairs={{0,28},{4,32},{8,36},{12,40},{16,44},{20,48},{24,52},{28,56},{32,6... | collective-permute-start | bytes 1544 | tf_op jit(solution)/shard_map/ppermute | solution.py:13
  153.2 17.6 %collective-permute-start.5 = (bf16[2,64,4,64]{3,1,2,0:T(8,128)(2,1)}, bf16[2,64,4,64]{3,1,2,0:T(8,128)(2,1)}, u32[]{:S(2)}, u32[]{:S(2)}) collective-permute-start(bf16[2,64,4,64]{3,1,2,0:T(8,128)(2,1)} %gather_fusion.2), channel_id=1, source_target_pairs={{0,8},{4,12},{8,16},{12,20},{16,24},{20,28},{24,32},{28,36},{32,40... | collective-permute-start | bytes 196616 | tf_op jit(solution)/shard_map/ppermute | solution.py:13
  154.6 18.1 %collective-permute-start.9 = (bf16[2,64,4,64]{3,1,2,0:T(8,128)(2,1)}, bf16[2,64,4,64]{3,1,2,0:T(8,128)(2,1)}, u32[]{:S(2)}, u32[]{:S(2)}) collective-permute-start(bf16[2,64,4,64]{3,1,2,0:T(8,128)(2,1)} %gather_fusion.2), channel_id=1, source_target_pairs={{0,12},{4,16},{8,20},{12,24},{16,28},{20,32},{24,36},{28,40},{32,4... | collective-permute-start | bytes 196616 | tf_op jit(solution)/shard_map/ppermute | solution.py:13
  154.7 22.1 %collective-permute-start.13 = (bf16[2,64,4,64]{3,1,2,0:T(8,128)(2,1)}, bf16[2,64,4,64]{3,1,2,0:T(8,128)(2,1)}, u32[]{:S(2)}, u32[]{:S(2)}) collective-permute-start(bf16[2,64,4,64]{3,1,2,0:T(8,128)(2,1)} %gather_fusion.2), channel_id=1, source_target_pairs={{0,16},{4,20},{8,24},{12,28},{16,32},{20,36},{24,40},{28,44},{32,4... | collective-permute-start | bytes 196616 | tf_op jit(solution)/shard_map/ppermute | solution.py:13
  156.9 25.3 %collective-permute-start.17 = (bf16[2,64,4,64]{3,1,2,0:T(8,128)(2,1)}, bf16[2,64,4,64]{3,1,2,0:T(8,128)(2,1)}, u32[]{:S(2)}, u32[]{:S(2)}) collective-permute-start(bf16[2,64,4,64]{3,1,2,0:T(8,128)(2,1)} %gather_fusion.2), channel_id=1, source_target_pairs={{0,20},{4,24},{8,28},{12,32},{16,36},{20,40},{24,44},{28,48},{32,5... | collective-permute-start | bytes 196616 | tf_op jit(solution)/shard_map/ppermute | solution.py:13
  158.4 29.3 %collective-permute-start.21 = (bf16[2,64,4,64]{3,1,2,0:T(8,128)(2,1)}, bf16[2,64,4,64]{3,1,2,0:T(8,128)(2,1)}, u32[]{:S(2)}, u32[]{:S(2)}) collective-permute-start(bf16[2,64,4,64]{3,1,2,0:T(8,128)(2,1)} %gather_fusion.2), channel_id=1, source_target_pairs={{0,24},{4,28},{8,32},{12,36},{16,40},{20,44},{24,48},{28,52},{32,5... | collective-permute-start | bytes 196616 | tf_op jit(solution)/shard_map/ppermute | solution.py:13
  170.1 9.5 %copy-start.16 = (bf16[2,128,1,256]{1,3,0,2:T(8,128)(2,1)S(1)}, bf16[2,128,1,256]{1,3,0,2:T(8,128)(2,1)}, u32[]{:S(2)}) copy-start(bf16[2,128,1,256]{1,3,0,2:T(8,128)(2,1)} %copy.184) | copy-start | bytes 393220
  170.1 10.7 %copy-start.22 = (bf16[2,128,1,256]{1,3,0,2:T(8,128)(2,1)S(1)}, bf16[2,128,1,256]{1,3,0,2:T(8,128)(2,1)}, u32[]{:S(2)}) copy-start(bf16[2,128,1,256]{1,3,0,2:T(8,128)(2,1)} %copy.183) | copy-start | bytes 393220
  170.8 18.4 %collective-permute-start.25 = (bf16[2,64,4,64]{3,1,2,0:T(8,128)(2,1)S(1)}, bf16[2,64,4,64]{3,1,2,0:T(8,128)(2,1)S(1)}, u32[]{:S(2)}, u32[]{:S(2)}) collective-permute-start(bf16[2,64,4,64]{3,1,2,0:T(8,128)(2,1)S(1)} %copy-done.31), channel_id=1, source_target_pairs={{0,28},{4,32},{8,36},{12,40},{16,44},{20,48},{24,52},{28,56},{32,6... | collective-permute-start | bytes 196616 | tf_op jit(solution)/shard_map/ppermute | solution.py:13
  171.0 14.2 %copy-start.15 = (bf16[2,128,1,256]{1,3,0,2:T(8,128)(2,1)S(1)}, bf16[2,128,1,256]{1,3,0,2:T(8,128)(2,1)}, u32[]{:S(2)}) copy-start(bf16[2,128,1,256]{1,3,0,2:T(8,128)(2,1)} %copy.189) | copy-start | bytes 393220
  172.2 14.2 %copy-start.21 = (bf16[2,128,1,256]{1,3,0,2:T(8,128)(2,1)S(1)}, bf16[2,128,1,256]{1,3,0,2:T(8,128)(2,1)}, u32[]{:S(2)}) copy-start(bf16[2,128,1,256]{1,3,0,2:T(8,128)(2,1)} %copy.188) | copy-start | bytes 393220
  172.8 20.0 %collective-permute-start.35 = (f32[2,4,64]{2,1,0:T(4,128)S(1)}, f32[2,4,64]{2,1,0:T(4,128)S(1)}, u32[]{:S(2)}, u32[]{:S(2)}) collective-permute-start(f32[2,4,64]{2,1,0:T(4,128)S(1)} %convert_reduce_fusion.8), channel_id=1, source_target_pairs={{0,248},{4,252},{8,0},{12,4},{16,8},{20,12},{24,16},{28,20},{32,24... | collective-permute-start | bytes 6152 | tf_op jit(solution)/shard_map/ppermute | solution.py:13
  174.9 12.8 %copy-start.14 = (bf16[2,128,1,256]{1,3,0,2:T(8,128)(2,1)S(1)}, bf16[2,128,1,256]{1,3,0,2:T(8,128)(2,1)}, u32[]{:S(2)}) copy-start(bf16[2,128,1,256]{1,3,0,2:T(8,128)(2,1)} %copy.194) | copy-start | bytes 393220
  176.4 15.8 %copy-start.13 = (bf16[2,128,1,256]{1,3,0,2:T(8,128)(2,1)S(1)}, bf16[2,128,1,256]{1,3,0,2:T(8,128)(2,1)}, u32[]{:S(2)}) copy-start(bf16[2,128,1,256]{1,3,0,2:T(8,128)(2,1)} %copy.199) | copy-start | bytes 393220
  176.7 16.7 %collective-permute-start.36 = (f32[2,4,64]{2,1,0:T(4,128)S(1)}, f32[2,4,64]{2,1,0:T(4,128)S(1)}, u32[]{:S(2)}, u32[]{:S(2)}) collective-permute-start(f32[2,4,64]{2,1,0:T(4,128)S(1)} %convert_reduce_fusion.7), channel_id=1, source_target_pairs={{0,244},{4,248},{8,252},{12,0},{16,4},{20,8},{24,12},{28,16},{32,2... | collective-permute-start | bytes 6152 | tf_op jit(solution)/shard_map/ppermute | solution.py:13
  180.8 21.5 %copy-start.20 = (bf16[2,128,1,256]{1,3,0,2:T(8,128)(2,1)S(1)}, bf16[2,128,1,256]{1,3,0,2:T(8,128)(2,1)}, u32[]{:S(2)}) copy-start(bf16[2,128,1,256]{1,3,0,2:T(8,128)(2,1)} %copy.193) | copy-start | bytes 393220
  181.9 27.9 %copy-start.19 = (bf16[2,128,1,256]{1,3,0,2:T(8,128)(2,1)S(1)}, bf16[2,128,1,256]{1,3,0,2:T(8,128)(2,1)}, u32[]{:S(2)}) copy-start(bf16[2,128,1,256]{1,3,0,2:T(8,128)(2,1)} %copy.198) | copy-start | bytes 393220
  182.1 15.5 %collective-permute-start.37 = (f32[2,4,64]{2,1,0:T(4,128)S(1)}, f32[2,4,64]{2,1,0:T(4,128)S(1)}, u32[]{:S(2)}, u32[]{:S(2)}) collective-permute-start(f32[2,4,64]{2,1,0:T(4,128)S(1)} %convert_reduce_fusion.6), channel_id=1, source_target_pairs={{0,240},{4,244},{8,248},{12,252},{16,0},{20,4},{24,8},{28,12},{32,... | collective-permute-start | bytes 6152 | tf_op jit(solution)/shard_map/ppermute | solution.py:13
  187.7 10.7 %collective-permute-start.38 = (f32[2,4,64]{2,1,0:T(4,128)S(1)}, f32[2,4,64]{2,1,0:T(4,128)S(1)}, u32[]{:S(2)}, u32[]{:S(2)}) collective-permute-start(f32[2,4,64]{2,1,0:T(4,128)S(1)} %convert_reduce_fusion.5), channel_id=1, source_target_pairs={{0,236},{4,240},{8,244},{12,248},{16,252},{20,0},{24,4},{28,8},{32... | collective-permute-start | bytes 6152 | tf_op jit(solution)/shard_map/ppermute | solution.py:13
  189.2 9.1 %collective-permute-start.39 = (f32[2,4,64]{2,1,0:T(4,128)S(1)}, f32[2,4,64]{2,1,0:T(4,128)S(1)}, u32[]{:S(2)}, u32[]{:S(2)}) collective-permute-start(f32[2,4,64]{2,1,0:T(4,128)S(1)} %convert_reduce_fusion.4), channel_id=1, source_target_pairs={{0,232},{4,236},{8,240},{12,244},{16,248},{20,252},{24,0},{28,4},{... | collective-permute-start | bytes 6152 | tf_op jit(solution)/shard_map/ppermute | solution.py:13
  192.8 11.3 %collective-permute-start.28 = (f32[2,4,64]{2,1,0:T(4,128)S(1)}, f32[2,4,64]{2,1,0:T(4,128)S(1)}, u32[]{:S(2)}, u32[]{:S(2)}) collective-permute-start(f32[2,4,64]{2,1,0:T(4,128)S(1)} %get-tuple-element.70), channel_id=1, source_target_pairs={{0,248},{4,252},{8,0},{12,4},{16,8},{20,12},{24,16},{28,20},{32,24... | collective-permute-start | bytes 6152 | tf_op jit(solution)/shard_map/ppermute | solution.py:13
  193.5 13.7 %collective-permute-start.29 = (f32[2,4,64]{2,1,0:T(4,128)S(1)}, f32[2,4,64]{2,1,0:T(4,128)S(1)}, u32[]{:S(2)}, u32[]{:S(2)}) collective-permute-start(f32[2,4,64]{2,1,0:T(4,128)S(1)} %get-tuple-element.72), channel_id=1, source_target_pairs={{0,244},{4,248},{8,252},{12,0},{16,4},{20,8},{24,12},{28,16},{32,2... | collective-permute-start | bytes 6152 | tf_op jit(solution)/shard_map/ppermute | solution.py:13
  197.6 9.6 %collective-permute-start.30 = (f32[2,4,64]{2,1,0:T(4,128)S(1)}, f32[2,4,64]{2,1,0:T(4,128)S(1)}, u32[]{:S(2)}, u32[]{:S(2)}) collective-permute-start(f32[2,4,64]{2,1,0:T(4,128)S(1)} %get-tuple-element.74), channel_id=1, source_target_pairs={{0,240},{4,244},{8,248},{12,252},{16,0},{20,4},{24,8},{28,12},{32,... | collective-permute-start | bytes 6152 | tf_op jit(solution)/shard_map/ppermute | solution.py:13
  198.4 10.2 %collective-permute-start.31 = (f32[2,4,64]{2,1,0:T(4,128)S(1)}, f32[2,4,64]{2,1,0:T(4,128)S(1)}, u32[]{:S(2)}, u32[]{:S(2)}) collective-permute-start(f32[2,4,64]{2,1,0:T(4,128)S(1)} %get-tuple-element.76), channel_id=1, source_target_pairs={{0,236},{4,240},{8,244},{12,248},{16,252},{20,0},{24,4},{28,8},{32... | collective-permute-start | bytes 6152 | tf_op jit(solution)/shard_map/ppermute | solution.py:13
  198.4 5.7 %collective-permute-start.40 = (f32[2,4,64]{2,1,0:T(4,128)S(1)}, f32[2,4,64]{2,1,0:T(4,128)S(1)}, u32[]{:S(2)}, u32[]{:S(2)}) collective-permute-start(f32[2,4,64]{2,1,0:T(4,128)S(1)} %convert_reduce_fusion.3), channel_id=1, source_target_pairs={{0,228},{4,232},{8,236},{12,240},{16,244},{20,248},{24,252},{28,0}... | collective-permute-start | bytes 6152 | tf_op jit(solution)/shard_map/ppermute | solution.py:13
  204.1 56.2 %collective-permute-start.1 = (bf16[8,64,4,64]{3,1,2,0:T(8,128)(2,1)}, bf16[8,64,4,64]{3,1,2,0:T(8,128)(2,1)}, u32[]{:S(2)}, u32[]{:S(2)}) collective-permute-start(bf16[8,64,4,64]{3,1,2,0:T(8,128)(2,1)} %copy.159), channel_id=1, source_target_pairs={{0,4},{4,8},{8,12},{12,16},{16,20},{20,24},{24,28},{28,32},{32,36}... | collective-permute-start | bytes 786440 | tf_op jit(solution)/shard_map/ppermute | solution.py:13
  204.1 6.7 %collective-permute-start.32 = (f32[2,4,64]{2,1,0:T(4,128)S(1)}, f32[2,4,64]{2,1,0:T(4,128)S(1)}, u32[]{:S(2)}, u32[]{:S(2)}) collective-permute-start(f32[2,4,64]{2,1,0:T(4,128)S(1)} %get-tuple-element.78), channel_id=1, source_target_pairs={{0,232},{4,236},{8,240},{12,244},{16,248},{20,252},{24,0},{28,4},{... | collective-permute-start | bytes 6152 | tf_op jit(solution)/shard_map/ppermute | solution.py:13
  207.2 5.9 %collective-permute-start.33 = (f32[2,4,64]{2,1,0:T(4,128)S(1)}, f32[2,4,64]{2,1,0:T(4,128)S(1)}, u32[]{:S(2)}, u32[]{:S(2)}) collective-permute-start(f32[2,4,64]{2,1,0:T(4,128)S(1)} %get-tuple-element.80), channel_id=1, source_target_pairs={{0,228},{4,232},{8,236},{12,240},{16,244},{20,248},{24,252},{28,0}... | collective-permute-start | bytes 6152 | tf_op jit(solution)/shard_map/ppermute | solution.py:13
  207.2 11.0 %collective-permute-start.6 = (f32[2,64,4,64]{1,3,2,0:T(8,128)S(1)}, f32[2,64,4,64]{1,3,2,0:T(8,128)S(1)}, u32[]{:S(2)}, u32[]{:S(2)}) collective-permute-start(f32[2,64,4,64]{1,3,2,0:T(8,128)S(1)} %convolution_bitcast_fusion.8), channel_id=1, source_target_pairs={{0,248},{4,252},{8,0},{12,4},{16,8},{20,12},{24,16},{28,20},{32,24... | collective-permute-start | bytes 393224 | tf_op jit(solution)/shard_map/ppermute | solution.py:13
  208.6 14.4 %collective-permute-start.10 = (f32[2,64,4,64]{1,3,2,0:T(8,128)S(1)}, f32[2,64,4,64]{1,3,2,0:T(8,128)S(1)}, u32[]{:S(2)}, u32[]{:S(2)}) collective-permute-start(f32[2,64,4,64]{1,3,2,0:T(8,128)S(1)} %convolution_bitcast_fusion.7), channel_id=1, source_target_pairs={{0,244},{4,248},{8,252},{12,0},{16,4},{20,8},{24,12},{28,16},{32,2... | collective-permute-start | bytes 393224 | tf_op jit(solution)/shard_map/ppermute | solution.py:13
  210.8 30.3 %collective-permute-start.14 = (f32[2,64,4,64]{1,3,2,0:T(8,128)}, f32[2,64,4,64]{1,3,2,0:T(8,128)}, u32[]{:S(2)}, u32[]{:S(2)}) collective-permute-start(f32[2,64,4,64]{1,3,2,0:T(8,128)} %convolution_bitcast_fusion.6), channel_id=1, source_target_pairs={{0,240},{4,244},{8,248},{12,252},{16,0},{20,4},{24,8},{28,12},{32,... | collective-permute-start | bytes 393224 | tf_op jit(solution)/shard_map/ppermute | solution.py:13
  213.1 32.8 %collective-permute-start.18 = (f32[2,64,4,64]{1,3,2,0:T(8,128)}, f32[2,64,4,64]{1,3,2,0:T(8,128)}, u32[]{:S(2)}, u32[]{:S(2)}) collective-permute-start(f32[2,64,4,64]{1,3,2,0:T(8,128)} %convolution_bitcast_fusion.5), channel_id=1, source_target_pairs={{0,236},{4,240},{8,244},{12,248},{16,252},{20,0},{24,4},{28,8},{32... | collective-permute-start | bytes 393224 | tf_op jit(solution)/shard_map/ppermute | solution.py:13
  218.2 32.5 %collective-permute-start.22 = (f32[2,64,4,64]{1,3,2,0:T(8,128)}, f32[2,64,4,64]{1,3,2,0:T(8,128)}, u32[]{:S(2)}, u32[]{:S(2)}) collective-permute-start(f32[2,64,4,64]{1,3,2,0:T(8,128)} %convolution_bitcast_fusion.4), channel_id=1, source_target_pairs={{0,232},{4,236},{8,240},{12,244},{16,248},{20,252},{24,0},{28,4},{... | collective-permute-start | bytes 393224 | tf_op jit(solution)/shard_map/ppermute | solution.py:13
  223.7 31.8 %collective-permute-start.26 = (f32[2,64,4,64]{1,3,2,0:T(8,128)}, f32[2,64,4,64]{1,3,2,0:T(8,128)}, u32[]{:S(2)}, u32[]{:S(2)}) collective-permute-start(f32[2,64,4,64]{1,3,2,0:T(8,128)} %convolution_bitcast_fusion.3), channel_id=1, source_target_pairs={{0,228},{4,232},{8,236},{12,240},{16,244},{20,248},{24,252},{28,0}... | collective-permute-start | bytes 393224 | tf_op jit(solution)/shard_map/ppermute | solution.py:13
  262.0 10.0 %copy-start.37 = (f32[8,4,64]{2,1,0:T(4,128)S(1)}, f32[8,4,64]{2,1,0:T(4,128)}, u32[]{:S(2)}) copy-start(f32[8,4,64]{2,1,0:T(4,128)} %copy-done.36) | copy-start | bytes 24580
  262.0 10.6 %copy-start.39 = (f32[8,4,64]{2,1,0:T(4,128)S(1)}, f32[8,4,64]{2,1,0:T(4,128)}, u32[]{:S(2)}) copy-start(f32[8,4,64]{2,1,0:T(4,128)} %copy-done.38) | copy-start | bytes 24580
  262.1 11.2 %copy-start.41 = (f32[8,4,64]{2,1,0:T(4,128)S(1)}, f32[8,4,64]{2,1,0:T(4,128)}, u32[]{:S(2)}) copy-start(f32[8,4,64]{2,1,0:T(4,128)} %copy-done.40) | copy-start | bytes 24580
  262.1 11.8 %copy-start.43 = (f32[8,4,64]{2,1,0:T(4,128)S(1)}, f32[8,4,64]{2,1,0:T(4,128)}, u32[]{:S(2)}) copy-start(f32[8,4,64]{2,1,0:T(4,128)} %copy-done.42) | copy-start | bytes 24580
  262.1 12.4 %copy-start.30 = (f32[9,8,4,64]{3,2,1,0:T(4,128)S(1)}, f32[9,8,4,64]{3,2,1,0:T(4,128)}, u32[]{:S(2)}) copy-start(f32[9,8,4,64]{3,2,1,0:T(4,128)} %constant_dynamic-update-slice_fusion.7) | copy-start | bytes 221188
  262.1 12.4 %collective-permute-start.27 = (f32[8,4,64]{2,1,0:T(4,128)S(1)}, f32[8,4,64]{2,1,0:T(4,128)S(1)}, u32[]{:S(2)}, u32[]{:S(2)}) collective-permute-start(f32[8,4,64]{2,1,0:T(4,128)S(1)} %get-tuple-element.68), channel_id=1, source_target_pairs={{0,252},{4,0},{8,4},{12,8},{16,12},{20,16},{24,20},{28,24},{32,28}... | collective-permute-start | bytes 24584 | tf_op jit(solution)/shard_map/ppermute | solution.py:13
  263.9 6.4 %collective-permute-start.34 = (f32[8,4,64]{2,1,0:T(4,128)S(1)}, f32[8,4,64]{2,1,0:T(4,128)S(1)}, u32[]{:S(2)}, u32[]{:S(2)}) collective-permute-start(f32[8,4,64]{2,1,0:T(4,128)S(1)} %convert_reduce_fusion), channel_id=1, source_target_pairs={{0,252},{4,0},{8,4},{12,8},{16,12},{20,16},{24,20},{28,24},{32,28}... | collective-permute-start | bytes 24584 | tf_op jit(solution)/shard_map/ppermute | solution.py:13
  265.6 18.1 %copy-start.2 = (f32[8,64,4,64]{1,3,2,0:T(8,128)S(1)}, f32[8,64,4,64]{1,3,2,0:T(8,128)}, u32[]{:S(2)}) copy-start(f32[8,64,4,64]{1,3,2,0:T(8,128)} %copy.176) | copy-start | bytes 1572868
  265.6 17.0 %collective-permute-start.2 = (f32[8,64,4,64]{1,3,2,0:T(8,128)S(1)}, f32[8,64,4,64]{1,3,2,0:T(8,128)S(1)}, u32[]{:S(2)}, u32[]{:S(2)}) collective-permute-start(f32[8,64,4,64]{1,3,2,0:T(8,128)S(1)} %convolution_bitcast_fusion), channel_id=1, source_target_pairs={{0,252},{4,0},{8,4},{12,8},{16,12},{20,16},{24,20},{28,24},{32,28}... | collective-permute-start | bytes 1572872 | tf_op jit(solution)/shard_map/ppermute | solution.py:13
  299.6 134.8 %reduce-scatter.2.cloned.1.call-start = ((), (), s32[]{:S(2)}) async-start(), calls=%async_computation.2 | async-start | bytes 1310720 | tf_op jit(solution)/shard_map/reduce_scatter | solution.py:168
  398.0 10.2 %copy-start.47 = (s32[8]{0:T(128)S(1)}, s32[8]{0:T(128)}, u32[]{:S(2)}) copy-start(s32[8]{0:T(128)} %param.23) | copy-start | bytes 100
  407.2 27.2 %copy-start.9 = (bf16[512,1024]{1,0:T(8,128)(2,1)S(1)}, bf16[512,1024]{1,0:T(8,128)(2,1)}, u32[]{:S(2)}) copy-start(bf16[512,1024]{1,0:T(8,128)(2,1)} %multiply_convert_fusion) | copy-start | bytes 3145732
  (28 other events, 118.6 us)
Sparse Core Ops, SparseCore 0:
  17.5 30.9 all-gather.3
  299.8 88.5 all-gather.5
  407.3 27.0 reduce-scatter.1
